TPU v7x, 32 devices: a whole 2x2x4 slice. The times are simulated.
32 devices in a mesh: vec: 16 (over z, y, x), row: 2 (over core).
Axes of the slice: x: 2, y: 2, z: 4, core: 2. Of those that a mesh axis runs over, the one named last changes fastest.
Arguments:
- vectors: bfloat16 [2, 4096, 1024], P('row', 'vec'), may hold values from -6 to 6
- rotation: bfloat16 [1024, 1024], P(None, 'vec'), may hold values from -0.1875 to 0.1875
- blocks: bfloat16 [64, 8, 128, 128], P('row'), may hold values from -0.125 to 0.125
- column_blocks: int32 [64, 8], P('row'), may hold values from -2 to 65, as said below
Outputs:
- filtered: bfloat16 [2, 4096, 1024], P('row', 'vec')
Inputs may be any that keep to these rules, and one draw needn't show every extreme that they name: `column_blocks`: block row r of partition p = r // 32 lists 8 distinct column blocks between p * 32 - 2 and p * 32 + 33; the first block row of every partition lists the lowest of these and the last one the highest; column blocks outside 0 to 63 stand for zeros.
All inputs are finite; a program needn't handle non-finite values.
Results may differ from a plain program's by a relative error of at most 0.006.
Values may be sent and summed in bfloat16 or wider, within the bound.
No kernel may reach another device: no remote copies, remote signals or barrier semaphores. Data moves between devices by JAX's collectives and lax.ppermute only.
A program may use at most 64 MiB of HBM per device.

v0:
```python
import functools

import jax
import jax.numpy as jnp
from jax import lax
from jax.experimental import pallas as pl
from jax.experimental.pallas import tpu as pltpu
from jax.sharding import PartitionSpec as P


HB = 2
STEPS = 4
PARTS = 2
LOADS = 3
TURNED = 4
DIRECT = 2

centre = 0.3
half_width = 1.2

VMEM = pl.BlockSpec(memory_space=pltpu.VMEM)
SMEM = pl.BlockSpec(memory_space=pltpu.SMEM)
ANY = pl.BlockSpec(memory_space=pl.ANY)


def in_hbm(array):
    return pltpu.with_memory_space_constraint(array, pltpu.HBM)


def identity(size):
    rows = lax.broadcasted_iota(jnp.int32, (size, size), 0)
    columns = lax.broadcasted_iota(jnp.int32, (size, size), 1)
    return (rows == columns).astype(jnp.bfloat16)


def turned_by(unit, block):
    return lax.dot_general(
        unit, block, (((1,), (1,)), ((), ())), preferred_element_type=jnp.float32
    ).astype(jnp.bfloat16)


def prepare_kernel(place, vectors, shard, sent, half, landing, leaving, arrived, left, picked):
    chunks, span, groups, columns, lanes = leaving.shape
    wide = span * columns
    fetch = [
        pltpu.make_async_copy(
            vectors.at[0, pl.ds(group * lanes, lanes)],
            landing.at[pl.ds(group * lanes, lanes)],
            arrived.at[group],
        )
        for group in range(groups)
    ]
    pick = pltpu.make_async_copy(
        shard.at[pl.ds(pl.multiple_of(place[1] * half.shape[1], half.shape[1]), half.shape[1])],
        half.at[0],
        picked,
    )
    for copy in fetch:
        copy.start()
    pick.start()
    unit = identity(wide)
    for copy in fetch:
        copy.wait()
    copies = []
    for chunk in range(chunks):
        turned = turned_by(unit, landing[:, chunk * wide : (chunk + 1) * wide])
        for group in range(groups):
            leaving[chunk, :, group] = turned[:, group * lanes : (group + 1) * lanes].reshape(
                span, columns, lanes
            )
        copies.append(
            pltpu.make_async_copy(
                leaving.at[chunk], sent.at[pl.ds(chunk * span, span)], left.at[chunk]
            )
        )
        copies[-1].start()
    pick.wait()
    for copy in copies:
        copy.wait()


def prepare(place, vectors, shard, groups, lanes):
    columns, total = shard.shape
    wide = max(columns, min(256, total))
    chunks, span = total // wide, wide // columns
    return pl.pallas_call(
        prepare_kernel,
        out_shape=(
            pltpu.HBM((total // columns, groups, columns, lanes), jnp.bfloat16),
            jax.ShapeDtypeStruct((1, columns // 2, total), jnp.bfloat16),
        ),
        in_specs=[SMEM, ANY, ANY],
        out_specs=(ANY, VMEM),
        scratch_shapes=[
            pltpu.VMEM((groups * lanes, total), jnp.bfloat16),
            pltpu.VMEM((chunks, span, groups, columns, lanes), jnp.bfloat16),
            pltpu.SemaphoreType.DMA((groups,)),
            pltpu.SemaphoreType.DMA((chunks,)),
            pltpu.SemaphoreType.DMA,
        ],
        compiler_params=pltpu.CompilerParams(vmem_limit_bytes=8 * 2**20),
        name="prepare",
    )(place, in_hbm(vectors), in_hbm(shard))


def turn_kernel(blocks, turned):
    rows, listed, width = blocks.shape[:3]
    unit = identity(2 * width)
    for row in range(0, rows, 2):
        for j in range(0, listed, 2):
            square = jnp.concatenate(
                [
                    jnp.concatenate([blocks[row + k, j], blocks[row + k, j + 1]], axis=1)
                    for k in range(2)
                ],
                axis=0,
            )
            turned[row // 2, j * width : (j + 2) * width, :] = turned_by(unit, square)


def turn_blocks(blocks, first, rows, space):
    listed, width = blocks.shape[1:3]
    skipped = first // TURNED
    size = rows * listed * width * width
    return pl.pallas_call(
        turn_kernel,
        grid=(rows // TURNED,),
        out_shape=space((rows // 2, listed * width, 2 * width), jnp.bfloat16),
        in_specs=[
            pl.BlockSpec((TURNED, listed, width, width), lambda row: (row + skipped, 0, 0, 0))
        ],
        out_specs=pl.BlockSpec((TURNED // 2, listed * width, 2 * width), lambda row: (row, 0, 0)),
        compiler_params=pltpu.CompilerParams(vmem_limit_bytes=16 * 2**20),
        cost_estimate=pl.CostEstimate(
            flops=4 * width * size, bytes_accessed=4 * size, transcendentals=0
        ),
        name="turn_blocks",
    )(in_hbm(blocks))


def step_kernel(first, last, count, place, listing, held, low, high, *refs):
    parts, refs = list(refs[:PARTS]), list(refs[PARTS:])
    moved = refs.pop()
    field = refs.pop()
    listed, rows = listing.shape
    chunk = rows // 2 // 4
    if first:
        source, parts[-1] = parts[-1], refs.pop()

        piece = source.shape[0] // LOADS

        def load(index):
            some = pl.ds(index * piece, piece)
            return pltpu.make_async_copy(source.at[some], parts[-1].at[some], moved.at[index])

        for index in range(LOADS):
            load(index).start()
        previous = current = held
    else:
        current, previous = refs[:2]
        refs = refs[2:]
    if last:
        result, operand = refs

        def store(index):
            some = pl.ds(index * 2 * chunk, 2 * chunk)
            return pltpu.make_async_copy(operand.at[some], result.at[some], moved.at[index])

    else:
        operand = refs[0]
    columns, width = held.shape[1:]
    shift = place[0] * rows - HB
    field[HB : HB + rows] = held[...]
    if count == 2:
        received = low[...]
        nothing = jnp.zeros_like(received)
        field[:HB] = jnp.where(place[0] == 1, received, nothing)
        field[HB + rows :] = jnp.where(place[0] == 0, received, nothing)
    else:
        field[:HB] = low[...]
        field[HB + rows :] = high[...]

    def picked(row):
        return jnp.concatenate([field[listing[j, row] - shift] for j in range(listed)], axis=1)

    def finish(row, product):
        if first:
            following = (product - centre * current[row].astype(jnp.float32)) / half_width
        else:
            following = (
                2.0 * (product - centre * current[row]) / half_width
                - previous[row].astype(jnp.float32)
            )
        operand[row] = following.astype(jnp.bfloat16)
        if not last:
            refs[1][row] = following

    def multiply(part, begin, end, pair):
        for index in range(begin, end):
            both = jnp.concatenate([picked(2 * pair), picked(2 * pair + 1)], axis=0)
            product = jnp.dot(both, part[index], preferred_element_type=jnp.float32)
            finish(2 * pair, product[:columns, :width])
            finish(2 * pair + 1, product[columns:, width:])
            pair += 1
            if last and pair % chunk == 0:
                store(pair // chunk - 1).start()

    ready = parts[0].shape[0]
    if first:
        here = place[0] >= 0
        pl.when(here)(lambda: multiply(parts[0], 0, ready, 0))
        for index in range(LOADS):
            load(index).wait()
            begin = index * piece
            pl.when(here)(
                functools.partial(multiply, parts[1], begin, begin + piece, ready + begin)
            )
    else:
        multiply(parts[0], 0, ready, 0)
        multiply(parts[1], 0, parts[1].shape[0], ready)
    if last:
        for index in range(4):
            store(index).wait()
    elif count == 2:
        start = jnp.where(place[0] == 0, rows - HB, 0)
        refs[2][...] = operand[pl.ds(start, HB)]
    else:
        refs[2][...] = operand[:HB]
        refs[3][...] = operand[rows - HB :]


def filter_step(turn, count, place, listing, held, halo, parts, state):
    first, last = turn == 0, turn == STEPS - 1
    rows, columns, width = held.shape
    edge = jax.ShapeDtypeStruct((HB, columns, width), jnp.bfloat16)
    parts = list(parts)
    tail = parts[-1]
    if first:
        parts[-1] = in_hbm(tail)
    args = [place, listing, held, *halo, *parts, *state]
    in_specs = [SMEM, SMEM] + [VMEM] * (len(args) - 2)
    scratch = [pltpu.VMEM((rows + 2 * HB, columns, width), jnp.bfloat16)]
    if last:
        out_shape = [pltpu.HBM(held.shape, jnp.bfloat16)]
        out_specs = [ANY]
        scratch = [pltpu.VMEM(held.shape, jnp.bfloat16)] + scratch
    else:
        out_shape = [
            jax.ShapeDtypeStruct(held.shape, jnp.bfloat16),
            jax.ShapeDtypeStruct(held.shape, jnp.float32),
        ]
        out_shape += [edge] if count == 2 else [edge, edge]
        if first:
            in_specs[5 + PARTS - 1] = ANY
            out_shape.append(jax.ShapeDtypeStruct(tail.shape, tail.dtype))
        out_specs = [VMEM] * len(out_shape)
    scratch.append(pltpu.SemaphoreType.DMA((4,)))
    size = sum(part.size for part in parts)
    return pl.pallas_call(
        functools.partial(step_kernel, first, last, count),
        out_shape=out_shape,
        in_specs=in_specs,
        out_specs=out_specs,
        scratch_shapes=scratch,
        compiler_params=pltpu.CompilerParams(vmem_limit_bytes=8 * 2**20),
        cost_estimate=pl.CostEstimate(
            flops=2 * size * columns, bytes_accessed=2 * size, transcendentals=0
        ),
        name="filter_step",
    )(*args)


def join_kernel(*refs):
    out = refs[-1]
    for index in range(out.shape[0]):
        out[index : index + 1] = refs[index][...]


def join(pieces, after):
    return pl.pallas_call(
        join_kernel,
        out_shape=jax.ShapeDtypeStruct((len(pieces),) + pieces[0].shape[1:], jnp.bfloat16),
        in_specs=[VMEM] * len(pieces) + [ANY],
        out_specs=VMEM,
        compiler_params=pltpu.CompilerParams(vmem_limit_bytes=2 * 2**20),
        name="join",
    )(*pieces, after)


def exchange(count, edges):
    if count == 2:
        received = lax.ppermute(edges[0], "row", [(0, 1), (1, 0)])
        return received, received
    first, last = edges
    forward = [(i, i + 1) for i in range(count - 1)]
    backward = [(i + 1, i) for i in range(count - 1)]
    return lax.ppermute(last, "row", forward), lax.ppermute(first, "row", backward)


def meet(array, code):
    pairs = [(i, i ^ code) for i in range(lax.axis_size("vec"))]
    return lax.ppermute(array, "vec", pairs)


def assemble_kernel(low, place, *refs):
    parts = 1 << low
    shards = refs[: 2 * parts]
    out, ordered = refs[2 * parts :]
    vec, _, half, total = ordered.shape
    side, me = place[1], place[2]
    for index in range(2 * parts):
        owner, part = index // parts, index % parts
        for slot in range(vec // parts):
            ordered[me ^ (slot << low | part), side ^ owner] = shards[index][slot]
    columns = 2 * half
    span = max(1, 256 // columns)
    wide = span * columns
    unit = identity(wide)
    for start in range(0, vec, span):
        rows = ordered[start : start + span].reshape(wide, total)
        for left in range(0, total, wide):
            out[left : left + wide, start * columns : (start + span) * columns] = turned_by(
                unit, rows[:, left : left + wide]
            )


def assemble(place, mine, theirs):
    parts = len(mine)
    slots, half, total = mine[0].shape
    return pl.pallas_call(
        functools.partial(assemble_kernel, parts.bit_length() - 1),
        out_shape=jax.ShapeDtypeStruct((total, total), jnp.bfloat16),
        in_specs=[SMEM] + [VMEM] * (2 * parts),
        out_specs=VMEM,
        scratch_shapes=[pltpu.VMEM((parts * slots, 2, half, total), jnp.bfloat16)],
        compiler_params=pltpu.CompilerParams(vmem_limit_bytes=8 * 2**20),
        cost_estimate=pl.CostEstimate(
            flops=512 * total * total, bytes_accessed=4 * total * total, transcendentals=0
        ),
        name="assemble",
    )(place, *mine, *theirs)


def rotate_kernel(filtered, rotation, out, rows, leaving, sent):
    _, groups, _, width = filtered.shape
    total = rotation.shape[0]
    wide = leaving.shape[2]
    unit = identity(width)
    for group in range(groups):
        turned = filtered[:, group].reshape(total, width)
        for start in range(0, total, wide):
            rows[group * width : (group + 1) * width, start : start + wide] = turned_by(
                unit, turned[start : start + wide]
            )
    copies = []
    for chunk in range(total // wide):
        some = slice(chunk * wide, (chunk + 1) * wide)
        leaving[chunk] = jnp.dot(
            rows[...], rotation[:, some], preferred_element_type=jnp.float32
        ).astype(jnp.bfloat16)
        copies.append(pltpu.make_async_copy(leaving.at[chunk], out.at[:, some], sent.at[chunk]))
        copies[-1].start()
    for copy in copies:
        copy.wait()


def rotate(filtered, rotation):
    vec, groups, columns, width = filtered.shape
    rows, total = groups * width, vec * columns
    wide = min(256, total)
    return pl.pallas_call(
        rotate_kernel,
        out_shape=pltpu.HBM((rows, total), jnp.bfloat16),
        in_specs=[VMEM, VMEM],
        out_specs=ANY,
        scratch_shapes=[
            pltpu.VMEM((rows, total), jnp.bfloat16),
            pltpu.VMEM((total // wide, rows, wide), jnp.bfloat16),
            pltpu.SemaphoreType.DMA((total // wide,)),
        ],
        compiler_params=pltpu.CompilerParams(vmem_limit_bytes=16 * 2**20),
        name="rotate",
    )(filtered, rotation)


def local(vectors, rotation, blocks, column_blocks):
    vec, count = lax.axis_size("vec"), lax.axis_size("row")
    rows, total = vectors.shape[1:]
    columns = total // vec
    width = blocks.shape[-1]
    lanes = min(rows, width)
    groups = rows // lanes
    part = width // lanes
    row = lax.axis_index("row")
    place = jnp.stack([row, row & 1, lax.axis_index("vec")]).astype(jnp.int32)
    listing = jnp.transpose(column_blocks)
    bits = vec.bit_length() - 1
    low = max(0, bits - DIRECT)

    sent, half = prepare(place, vectors, jnp.transpose(rotation), groups, lanes)
    got = lax.all_to_all(sent, "vec", split_axis=0, concat_axis=0, tiled=True)
    pieces = [half]
    for code in range(1, vec >> low):
        if code == 3:
            pieces.append(meet(pieces[2], 1 << low))
        else:
            pieces.append(meet(half, code << low))
    quarter = blocks.shape[0] // 4
    tail = turn_blocks(blocks, quarter, 3 * quarter, pltpu.HBM)
    head = turn_blocks(blocks, 0, quarter, jax.ShapeDtypeStruct)
    held = got.reshape(-1, part, columns, lanes).swapaxes(1, 2).reshape(-1, columns, width)

    if count == 2:
        start = jnp.where(row == 0, held.shape[0] - HB, 0)
        edges = [lax.dynamic_slice_in_dim(held, start, HB)]
    else:
        edges = [held[:HB], held[held.shape[0] - HB :]]
    mine = [join(pieces, edges[0])]
    operand, state = held, ()
    older, newer = None, held
    parts = [head, tail]
    for turn in range(STEPS):
        halo = exchange(count, edges)
        outs = filter_step(turn, count, place, listing, operand, halo, parts, state)
        operand = outs[0]
        if turn == 0:
            outs, parts[-1] = outs[:-1], outs[-1]
        if turn < STEPS - 1:
            edges = outs[2 : 3 if count == 2 else 4]
            older, newer = newer, outs[1]
            state = (newer, older)
    for bit in range(low):
        more = []
        for array in mine:
            more.append(meet(array, 1 << bit))
        mine += more

    back = operand.reshape(-1, columns, part, lanes).swapaxes(1, 2)
    back = back.reshape(vec, groups, columns, lanes)
    returned = lax.all_to_all(back, "vec", split_axis=0, concat_axis=0, tiled=True)
    theirs = []
    for array in mine:
        theirs.append(lax.ppermute(array, "row", [(i, i ^ 1) for i in range(count)]))
    rotation = assemble(place, mine, theirs)
    return rotate(returned, rotation)[None]


def solution(mesh):
    placed = (P("row", "vec", None), P(None, "vec"), P("row", None, None, None), P("row", None))

    return jax.shard_map(
        local, mesh=mesh, in_specs=placed, out_specs=P("row", "vec", None), check_vma=False
    )
```

profile of v0, /device:TPU:0, one launch (start us, length us, event | category | flops | bytes accessed | tf_op | source)
XLA Modules:
  0.0 87.4 jit_solution(15575692722318747268)
XLA Ops:
  0.0 0.1 pad_add_fusion.place
  0.1 2.7 %prepare.1 = (bf16[16,2,64,128]{3,2,1,0:T(8,128)(2,1)}, bf16[1,32,1024]{2,1,0:T(8,128)(2,1)S(1)}) custom-call(s32[3]{0:T(128)S(1)} %pad_add_fusion.place, bf16[1,256,1024]{2,1,0:T(8,128)(2,1)} %vectors.1, bf16[64,1024]{1,0:T(8,128)(2,1)} %bitcast.16), custom_call_target="tpu_custom_call" | custom-call | tf_op jit(solution)/shard_map/prepare/pallas_call | solution.py:86
  2.8 8.4 %all-to-all-start = ((bf16[16,2,64,128]{3,2,1,0:T(8,128)(2,1)}), bf16[16,2,64,128]{3,2,1,0:T(8,128)(2,1)S(1)}, u32[]{:S(2)}, u32[]{:S(2)}) async-start(bf16[16,2,64,128]{3,2,1,0:T(8,128)(2,1)} %get-tuple-element.17), calls=%async_computation | async-start | bytes 1048576 | tf_op jit(solution)/shard_map/all_to_all | solution.py:401
  11.1 8.1 %turn_blocks.3.refs_1_ = bf16[12,1024,256]{2,1,0:T(8,128)(2,1)} custom-call(bf16[32,8,128,128]{3,2,1,0:T(8,128)(2,1)} %blocks.3), custom_call_target="tpu_custom_call" | custom-call | flops 1610612736 | bytes 12582912 | tf_op jit(solution)/shard_map/turn_blocks/pallas_call | solution.py:125
  19.3 6.9 %all-to-all-done = bf16[16,2,64,128]{3,2,1,0:T(8,128)(2,1)S(1)} async-done(((bf16[16,2,64,128]{3,2,1,0:T(8,128)(2,1)}), bf16[16,2,64,128]{3,2,1,0:T(8,128)(2,1)S(1)}, u32[]{:S(2)}, u32[]{:S(2)}) %all-to-all-start) | async-done | bytes 524320 | tf_op jit(solution)/shard_map/all_to_all | solution.py:401
  26.2 0.0 collective-permute-start
  26.2 2.2 %turn_blocks.2.refs_0_ = bf16[4,1024,256]{2,1,0:T(8,128)(2,1)S(1)} custom-call(bf16[32,8,128,128]{3,2,1,0:T(8,128)(2,1)} %blocks.3), custom_call_target="tpu_custom_call" | custom-call | flops 536870912 | bytes 4194304 | tf_op jit(solution)/shard_map/turn_blocks/pallas_call | solution.py:125
  28.4 4.0 %filter_step.4 = (bf16[32,64,128]{2,1,0:T(8,128)(2,1)S(1)}, f32[32,64,128]{2,1,0:T(8,128)S(1)}, bf16[2,64,128]{2,1,0:T(8,128)(2,1)S(1)}, bf16[12,1024,256]{2,1,0:T(8,128)(2,1)S(1)}) custom-call(s32[3]{0:T(128)S(1)} %pad_add_fusion.place, s32[8,32]{1,0:T(8,128)S(1)} %bitcast.11, bf16[32,64,128]{2,1,0:T(8,128)(2,1)S(1)} %bitcast.9, ...), custom_call_target="tpu_custom_call" | custom-call | flops 536870912 | bytes 8388608 | tf_op jit(solution)/shard_map/filter_step/pallas_call | solution.py:259
  32.4 0.6 collective-permute-start.1
  33.0 0.9 collective-permute-done.1.low.high
  33.8 2.1 %filter_step.5 = (bf16[32,64,128]{2,1,0:T(8,128)(2,1)S(1)}, f32[32,64,128]{2,1,0:T(8,128)S(1)}, bf16[2,64,128]{2,1,0:T(8,128)(2,1)S(1)}) custom-call(s32[3]{0:T(128)S(1)} %pad_add_fusion.place, s32[8,32]{1,0:T(8,128)S(1)} %bitcast.12, bf16[32,64,128]{2,1,0:T(8,128)(2,1)S(1)} %get-tuple-element.18.held, ...), custom_call_target="tpu_custom_call" | custom-call | flops 536870912 | bytes 8388608 | tf_op jit(solution)/shard_map/filter_step/pallas_call | solution.py:259
  35.9 0.4 collective-permute-start.2
  36.3 0.9 %collective-permute-done.2.low.high = bf16[2,64,128]{2,1,0:T(8,128)(2,1)S(1)} collective-permute-done((bf16[2,64,128]{2,1,0:T(8,128)(2,1)S(1)}, bf16[2,64,128]{2,1,0:T(8,128)(2,1)S(1)}, u32[]{:S(2)}, u32[]{:S(2)}) %collective-permute-start.2) | collective-permute-done | bytes 32800 | tf_op jit(solution)/shard_map/ppermute | solution.py:292
  37.2 2.1 %filter_step.6 = (bf16[32,64,128]{2,1,0:T(8,128)(2,1)S(1)}, f32[32,64,128]{2,1,0:T(8,128)S(1)}, bf16[2,64,128]{2,1,0:T(8,128)(2,1)S(1)}) custom-call(s32[3]{0:T(128)S(1)} %pad_add_fusion.place, s32[8,32]{1,0:T(8,128)S(1)} %bitcast.13, bf16[32,64,128]{2,1,0:T(8,128)(2,1)S(1)} %get-tuple-element.22.held, ...), custom_call_target="tpu_custom_call" | custom-call | flops 536870912 | bytes 8388608 | tf_op jit(solution)/shard_map/filter_step/pallas_call | solution.py:259
  39.3 0.4 collective-permute-start.3
  39.7 0.9 %collective-permute-done.3.low.high = bf16[2,64,128]{2,1,0:T(8,128)(2,1)S(1)} collective-permute-done((bf16[2,64,128]{2,1,0:T(8,128)(2,1)S(1)}, bf16[2,64,128]{2,1,0:T(8,128)(2,1)S(1)}, u32[]{:S(2)}, u32[]{:S(2)}) %collective-permute-start.3) | collective-permute-done | bytes 32800 | tf_op jit(solution)/shard_map/ppermute | solution.py:292
  40.6 2.7 %filter_step.7 = bf16[32,64,128]{2,1,0:T(8,128)(2,1)} custom-call(s32[3]{0:T(128)S(1)} %pad_add_fusion.place, s32[8,32]{1,0:T(8,128)S(1)} %bitcast.14, bf16[32,64,128]{2,1,0:T(8,128)(2,1)S(1)} %get-tuple-element.25.held, bf16[2,64,128]{2,1,0:T(8,128)(2,1)S(1)} %collective-permute-done.3.low.high, bf16[2,64,128]{2,1,0:T(8,128)(2,1)S(1)} %collective-permute-done.3.low.high, ...), custom_call_target="tpu_custom_call" | custom-call | flops 536870912 | bytes 8388608 | tf_op jit(solution)/shard_map/filter_step/pallas_call | solution.py:259
  43.3 4.0 %all-to-all-start.1 = ((bf16[16,2,64,128]{3,2,1,0:T(8,128)(2,1)}), bf16[16,2,64,128]{3,2,1,0:T(8,128)(2,1)S(1)}, u32[]{:S(2)}, u32[]{:S(2)}) async-start(bf16[16,2,64,128]{3,2,1,0:T(8,128)(2,1)} %bitcast.15), calls=%async_computation.1 | async-start | bytes 1048576 | tf_op jit(solution)/shard_map/all_to_all | solution.py:440
  47.3 2.8 %collective-permute-start.5 = (bf16[1,32,1024]{2,1,0:T(8,128)(2,1)S(1)}, bf16[1,32,1024]{2,1,0:T(8,128)(2,1)S(1)}, u32[]{:S(2)}, u32[]{:S(2)}) collective-permute-start(bf16[1,32,1024]{2,1,0:T(8,128)(2,1)S(1)} %get-tuple-element.28.refs_0_), channel_id=1, source_target_pairs={{0,16},{2,18},{4,20},{6,22},{8,24},{10,26},{12,28},{14,30},{16,0},... | collective-permute-start | bytes 196616 | tf_op jit(solution)/shard_map/ppermute | solution.py:302
  50.1 1.5 %collective-permute-start.4 = (bf16[1,32,1024]{2,1,0:T(8,128)(2,1)S(1)}, bf16[1,32,1024]{2,1,0:T(8,128)(2,1)S(1)}, u32[]{:S(2)}, u32[]{:S(2)}) collective-permute-start(bf16[1,32,1024]{2,1,0:T(8,128)(2,1)S(1)} %get-tuple-element.28.refs_0_), channel_id=1, source_target_pairs={{0,8},{2,10},{4,12},{6,14},{8,0},{10,2},{12,4},{14,6},{16,24},{18,... | collective-permute-start | bytes 196616 | tf_op jit(solution)/shard_map/ppermute | solution.py:302
  51.6 13.4 %collective-permute-done.5.refs_2_ = bf16[1,32,1024]{2,1,0:T(8,128)(2,1)S(1)} collective-permute-done((bf16[1,32,1024]{2,1,0:T(8,128)(2,1)S(1)}, bf16[1,32,1024]{2,1,0:T(8,128)(2,1)S(1)}, u32[]{:S(2)}, u32[]{:S(2)}) %collective-permute-start.5) | collective-permute-done | bytes 65568 | tf_op jit(solution)/shard_map/ppermute | solution.py:302
  65.0 4.3 %collective-permute-done.6.refs_3_ = bf16[1,32,1024]{2,1,0:T(8,128)(2,1)S(1)} collective-permute-done((bf16[1,32,1024]{2,1,0:T(8,128)(2,1)S(1)}, bf16[1,32,1024]{2,1,0:T(8,128)(2,1)S(1)}, u32[]{:S(2)}, u32[]{:S(2)}) %collective-permute-start.6) | collective-permute-done | bytes 65568 | tf_op jit(solution)/shard_map/ppermute | solution.py:302
  69.2 1.5 %collective-permute-start.7 = (bf16[4,32,1024]{2,1,0:T(8,128)(2,1)S(1)}, bf16[4,32,1024]{2,1,0:T(8,128)(2,1)S(1)}, u32[]{:S(2)}, u32[]{:S(2)}) collective-permute-start(bf16[4,32,1024]{2,1,0:T(8,128)(2,1)S(1)} %join.1.refs_0_), channel_id=1, source_target_pairs={{0,2},{2,0},{4,6},{6,4},{8,10},{10,8},{12,14},{14,12},{16,18},{18,... | collective-permute-start | bytes 786440 | tf_op jit(solution)/shard_map/ppermute | solution.py:302
  70.8 1.5 %collective-permute-start.8 = (bf16[4,32,1024]{2,1,0:T(8,128)(2,1)S(1)}, bf16[4,32,1024]{2,1,0:T(8,128)(2,1)S(1)}, u32[]{:S(2)}, u32[]{:S(2)}) collective-permute-start(bf16[4,32,1024]{2,1,0:T(8,128)(2,1)S(1)} %join.1.refs_0_), channel_id=1, source_target_pairs={{0,4},{2,6},{4,0},{6,2},{8,12},{10,14},{12,8},{14,10},{16,20},{18,... | collective-permute-start | bytes 786440 | tf_op jit(solution)/shard_map/ppermute | solution.py:302
  72.2 3.4 %collective-permute-done.7.refs_1_ = bf16[4,32,1024]{2,1,0:T(8,128)(2,1)S(1)} collective-permute-done((bf16[4,32,1024]{2,1,0:T(8,128)(2,1)S(1)}, bf16[4,32,1024]{2,1,0:T(8,128)(2,1)S(1)}, u32[]{:S(2)}, u32[]{:S(2)}) %collective-permute-start.7) | collective-permute-done | bytes 262176 | tf_op jit(solution)/shard_map/ppermute | solution.py:302
  75.7 1.5 %collective-permute-start.9 = (bf16[4,32,1024]{2,1,0:T(8,128)(2,1)S(1)}, bf16[4,32,1024]{2,1,0:T(8,128)(2,1)S(1)}, u32[]{:S(2)}, u32[]{:S(2)}) collective-permute-start(bf16[4,32,1024]{2,1,0:T(8,128)(2,1)S(1)} %collective-permute-done.7.refs_1_), channel_id=1, source_target_pairs={{0,4},{2,6},{4,0},{6,2},{8,12},{10,14},{12,8},{14,10},{16,20},{18,... | collective-permute-start | bytes 786440 | tf_op jit(solution)/shard_map/ppermute | solution.py:302
  77.1 0.5 collective-permute-start.11
  77.6 1.6 %collective-permute-done.8.refs_2_ = bf16[4,32,1024]{2,1,0:T(8,128)(2,1)S(1)} collective-permute-done((bf16[4,32,1024]{2,1,0:T(8,128)(2,1)S(1)}, bf16[4,32,1024]{2,1,0:T(8,128)(2,1)S(1)}, u32[]{:S(2)}, u32[]{:S(2)}) %collective-permute-start.8) | collective-permute-done | bytes 262176 | tf_op jit(solution)/shard_map/ppermute | solution.py:302
  79.2 3.5 %collective-permute-done.9.refs_3_ = bf16[4,32,1024]{2,1,0:T(8,128)(2,1)S(1)} collective-permute-done((bf16[4,32,1024]{2,1,0:T(8,128)(2,1)S(1)}, bf16[4,32,1024]{2,1,0:T(8,128)(2,1)S(1)}, u32[]{:S(2)}, u32[]{:S(2)}) %collective-permute-start.9) | collective-permute-done | bytes 262176 | tf_op jit(solution)/shard_map/ppermute | solution.py:302
  82.8 1.5 %collective-permute-done.13.refs_7_ = bf16[4,32,1024]{2,1,0:T(8,128)(2,1)S(1)} collective-permute-done((bf16[4,32,1024]{2,1,0:T(8,128)(2,1)S(1)}, bf16[4,32,1024]{2,1,0:T(8,128)(2,1)S(1)}, u32[]{:S(2)}, u32[]{:S(2)}) %collective-permute-start.13) | collective-permute-done | bytes 262176 | tf_op jit(solution)/shard_map/ppermute | solution.py:443
  84.3 1.4 %assemble.1.rotation = bf16[1024,1024]{1,0:T(8,128)(2,1)S(1)} custom-call(s32[3]{0:T(128)S(1)} %pad_add_fusion.place, bf16[4,32,1024]{2,1,0:T(8,128)(2,1)S(1)} %join.1.refs_0_, bf16[4,32,1024]{2,1,0:T(8,128)(2,1)S(1)} %collective-permute-done.7.refs_1_, bf16[4,32,1024]{2,1,0:T(8,128)(2,1)S(1)} %collective-permute-done.8.refs_2_, ...), custom_call_target="tpu_custom_call" | custom-call | flops 536870912 | bytes 4194304 | tf_op jit(solution)/shard_map/assemble/pallas_call | solution.py:330
  85.7 1.6 %rotate.1 = bf16[256,1024]{1,0:T(8,128)(2,1)} custom-call(bf16[16,2,64,128]{3,2,1,0:T(8,128)(2,1)S(1)} %all-to-all-done.1.filtered, bf16[1024,1024]{1,0:T(8,128)(2,1)S(1)} %assemble.1.rotation), custom_call_target="tpu_custom_call" | custom-call | tf_op jit(solution)/shard_map/rotate/pallas_call | solution.py:371
  (14 shorter events, 0.1 us)
Async XLA Ops:
  2.8 23.4 %all-to-all-start = ((bf16[16,2,64,128]{3,2,1,0:T(8,128)(2,1)}), bf16[16,2,64,128]{3,2,1,0:T(8,128)(2,1)S(1)}, u32[]{:S(2)}, u32[]{:S(2)}) async-start(bf16[16,2,64,128]{3,2,1,0:T(8,128)(2,1)} %get-tuple-element.17), calls=%async_computation | async-start | bytes 1048576 | tf_op jit(solution)/shard_map/all_to_all | solution.py:401
  19.3 9.2 %copy-start = (s32[32,8]{0,1:T(8,128)S(1)}, s32[32,8]{0,1:T(8,128)}, u32[]{:S(2)}) copy-start(s32[32,8]{0,1:T(8,128)} %param.7) | copy-start | bytes 3076
  26.2 2.2 %collective-permute-start = (bf16[2,64,128]{2,1,0:T(8,128)(2,1)S(1)}, bf16[2,64,128]{2,1,0:T(8,128)(2,1)S(1)}, u32[]{:S(2)}, u32[]{:S(2)}) collective-permute-start(bf16[2,64,128]{2,1,0:T(8,128)(2,1)S(1)} %constant_dynamic-slice_fusion.refs_4_), channel_id=1, source_target_pairs={{0,1},{1,0},{2,3},{3,2},{4,5},{5,4},{6,7},{7,6},{8,9},{9,8},{10,11... | collective-permute-start | bytes 98312 | tf_op jit(solution)/shard_map/ppermute | solution.py:292
  32.4 1.4 %collective-permute-start.1 = (bf16[2,64,128]{2,1,0:T(8,128)(2,1)S(1)}, bf16[2,64,128]{2,1,0:T(8,128)(2,1)S(1)}, u32[]{:S(2)}, u32[]{:S(2)}) collective-permute-start(bf16[2,64,128]{2,1,0:T(8,128)(2,1)S(1)} %get-tuple-element.19), channel_id=1, source_target_pairs={{0,1},{1,0},{2,3},{3,2},{4,5},{5,4},{6,7},{7,6},{8,9},{9,8},{10,11... | collective-permute-start | bytes 98312 | tf_op jit(solution)/shard_map/ppermute | solution.py:292
  35.9 1.3 %collective-permute-start.2 = (bf16[2,64,128]{2,1,0:T(8,128)(2,1)S(1)}, bf16[2,64,128]{2,1,0:T(8,128)(2,1)S(1)}, u32[]{:S(2)}, u32[]{:S(2)}) collective-permute-start(bf16[2,64,128]{2,1,0:T(8,128)(2,1)S(1)} %get-tuple-element.23), channel_id=1, source_target_pairs={{0,1},{1,0},{2,3},{3,2},{4,5},{5,4},{6,7},{7,6},{8,9},{9,8},{10,11... | collective-permute-start | bytes 98312 | tf_op jit(solution)/shard_map/ppermute | solution.py:292
  39.3 1.3 %collective-permute-start.3 = (bf16[2,64,128]{2,1,0:T(8,128)(2,1)S(1)}, bf16[2,64,128]{2,1,0:T(8,128)(2,1)S(1)}, u32[]{:S(2)}, u32[]{:S(2)}) collective-permute-start(bf16[2,64,128]{2,1,0:T(8,128)(2,1)S(1)} %get-tuple-element.26), channel_id=1, source_target_pairs={{0,1},{1,0},{2,3},{3,2},{4,5},{5,4},{6,7},{7,6},{8,9},{9,8},{10,11... | collective-permute-start | bytes 98312 | tf_op jit(solution)/shard_map/ppermute | solution.py:292
  43.3 42.4 %all-to-all-start.1 = ((bf16[16,2,64,128]{3,2,1,0:T(8,128)(2,1)}), bf16[16,2,64,128]{3,2,1,0:T(8,128)(2,1)S(1)}, u32[]{:S(2)}, u32[]{:S(2)}) async-start(bf16[16,2,64,128]{3,2,1,0:T(8,128)(2,1)} %bitcast.15), calls=%async_computation.1 | async-start | bytes 1048576 | tf_op jit(solution)/shard_map/all_to_all | solution.py:440
  47.3 17.7 %collective-permute-start.5 = (bf16[1,32,1024]{2,1,0:T(8,128)(2,1)S(1)}, bf16[1,32,1024]{2,1,0:T(8,128)(2,1)S(1)}, u32[]{:S(2)}, u32[]{:S(2)}) collective-permute-start(bf16[1,32,1024]{2,1,0:T(8,128)(2,1)S(1)} %get-tuple-element.28.refs_0_), channel_id=1, source_target_pairs={{0,16},{2,18},{4,20},{6,22},{8,24},{10,26},{12,28},{14,30},{16,0},... | collective-permute-start | bytes 196616 | tf_op jit(solution)/shard_map/ppermute | solution.py:302
  50.1 14.9 %collective-permute-start.4 = (bf16[1,32,1024]{2,1,0:T(8,128)(2,1)S(1)}, bf16[1,32,1024]{2,1,0:T(8,128)(2,1)S(1)}, u32[]{:S(2)}, u32[]{:S(2)}) collective-permute-start(bf16[1,32,1024]{2,1,0:T(8,128)(2,1)S(1)} %get-tuple-element.28.refs_0_), channel_id=1, source_target_pairs={{0,8},{2,10},{4,12},{6,14},{8,0},{10,2},{12,4},{14,6},{16,24},{18,... | collective-permute-start | bytes 196616 | tf_op jit(solution)/shard_map/ppermute | solution.py:302
  64.9 4.3 %collective-permute-start.6 = (bf16[1,32,1024]{2,1,0:T(8,128)(2,1)S(1)}, bf16[1,32,1024]{2,1,0:T(8,128)(2,1)S(1)}, u32[]{:S(2)}, u32[]{:S(2)}) collective-permute-start(bf16[1,32,1024]{2,1,0:T(8,128)(2,1)S(1)} %collective-permute-done.5.refs_2_), channel_id=1, source_target_pairs={{0,8},{2,10},{4,12},{6,14},{8,0},{10,2},{12,4},{14,6},{16,24},{18,... | collective-permute-start | bytes 196616 | tf_op jit(solution)/shard_map/ppermute | solution.py:302
  69.2 6.4 %collective-permute-start.7 = (bf16[4,32,1024]{2,1,0:T(8,128)(2,1)S(1)}, bf16[4,32,1024]{2,1,0:T(8,128)(2,1)S(1)}, u32[]{:S(2)}, u32[]{:S(2)}) collective-permute-start(bf16[4,32,1024]{2,1,0:T(8,128)(2,1)S(1)} %join.1.refs_0_), channel_id=1, source_target_pairs={{0,2},{2,0},{4,6},{6,4},{8,10},{10,8},{12,14},{14,12},{16,18},{18,... | collective-permute-start | bytes 786440 | tf_op jit(solution)/shard_map/ppermute | solution.py:302
  70.8 8.5 %collective-permute-start.8 = (bf16[4,32,1024]{2,1,0:T(8,128)(2,1)S(1)}, bf16[4,32,1024]{2,1,0:T(8,128)(2,1)S(1)}, u32[]{:S(2)}, u32[]{:S(2)}) collective-permute-start(bf16[4,32,1024]{2,1,0:T(8,128)(2,1)S(1)} %join.1.refs_0_), channel_id=1, source_target_pairs={{0,4},{2,6},{4,0},{6,2},{8,12},{10,14},{12,8},{14,10},{16,20},{18,... | collective-permute-start | bytes 786440 | tf_op jit(solution)/shard_map/ppermute | solution.py:302
  75.7 7.1 %collective-permute-start.9 = (bf16[4,32,1024]{2,1,0:T(8,128)(2,1)S(1)}, bf16[4,32,1024]{2,1,0:T(8,128)(2,1)S(1)}, u32[]{:S(2)}, u32[]{:S(2)}) collective-permute-start(bf16[4,32,1024]{2,1,0:T(8,128)(2,1)S(1)} %collective-permute-done.7.refs_1_), channel_id=1, source_target_pairs={{0,4},{2,6},{4,0},{6,2},{8,12},{10,14},{12,8},{14,10},{16,20},{18,... | collective-permute-start | bytes 786440 | tf_op jit(solution)/shard_map/ppermute | solution.py:302
  77.1 5.6 %collective-permute-start.10 = (bf16[4,32,1024]{2,1,0:T(8,128)(2,1)S(1)}, bf16[4,32,1024]{2,1,0:T(8,128)(2,1)S(1)}, u32[]{:S(2)}, u32[]{:S(2)}) collective-permute-start(bf16[4,32,1024]{2,1,0:T(8,128)(2,1)S(1)} %join.1.refs_0_), channel_id=1, source_target_pairs={{0,1},{1,0},{2,3},{3,2},{4,5},{5,4},{6,7},{7,6},{8,9},{9,8},{10,11... | collective-permute-start | bytes 786440 | tf_op jit(solution)/shard_map/ppermute | solution.py:443
  77.1 5.6 %collective-permute-start.11 = (bf16[4,32,1024]{2,1,0:T(8,128)(2,1)S(1)}, bf16[4,32,1024]{2,1,0:T(8,128)(2,1)S(1)}, u32[]{:S(2)}, u32[]{:S(2)}) collective-permute-start(bf16[4,32,1024]{2,1,0:T(8,128)(2,1)S(1)} %collective-permute-done.7.refs_1_), channel_id=1, source_target_pairs={{0,1},{1,0},{2,3},{3,2},{4,5},{5,4},{6,7},{7,6},{8,9},{9,8},{10,11... | collective-permute-start | bytes 786440 | tf_op jit(solution)/shard_map/ppermute | solution.py:443
  79.2 3.5 %collective-permute-start.12 = (bf16[4,32,1024]{2,1,0:T(8,128)(2,1)S(1)}, bf16[4,32,1024]{2,1,0:T(8,128)(2,1)S(1)}, u32[]{:S(2)}, u32[]{:S(2)}) collective-permute-start(bf16[4,32,1024]{2,1,0:T(8,128)(2,1)S(1)} %collective-permute-done.8.refs_2_), channel_id=1, source_target_pairs={{0,1},{1,0},{2,3},{3,2},{4,5},{5,4},{6,7},{7,6},{8,9},{9,8},{10,11... | collective-permute-start | bytes 786440 | tf_op jit(solution)/shard_map/ppermute | solution.py:443
  82.8 1.5 %collective-permute-start.13 = (bf16[4,32,1024]{2,1,0:T(8,128)(2,1)S(1)}, bf16[4,32,1024]{2,1,0:T(8,128)(2,1)S(1)}, u32[]{:S(2)}, u32[]{:S(2)}) collective-permute-start(bf16[4,32,1024]{2,1,0:T(8,128)(2,1)S(1)} %collective-permute-done.9.refs_3_), channel_id=1, source_target_pairs={{0,1},{1,0},{2,3},{3,2},{4,5},{5,4},{6,7},{7,6},{8,9},{9,8},{10,11... | collective-permute-start | bytes 786440 | tf_op jit(solution)/shard_map/ppermute | solution.py:443
where the time goes:
time: 87.8 us; the launch traced here: 87.4 us
  waiting for transfers between devices  37.3 us (42%)
  Pallas kernels  26.9 us (31%)
  starting transfers between devices  22.9 us (26%)
    ppermute x6, waiting for transfers between devices, meet(): return lax.ppermute(array, 'vec', pairs)  26.2 us
    pallas_call x4, Pallas kernels, filter_step(): pl.pallas_call(functools.partial(step_kernel, first, last, count), out_sh...  10.9 us
    pallas_call x2, Pallas kernels, turn_blocks(): pl.pallas_call(turn_kernel, grid=(rows // TURNED,), out_shape=space((rows...  10.3 us
    ppermute x6, starting transfers between devices, meet(): return lax.ppermute(array, 'vec', pairs)  8.75 us
    all_to_all x1, starting transfers between devices, local(): got = lax.all_to_all(sent, 'vec', split_axis=0, concat_axis=0, tiled=True)  8.36 us
    all_to_all x1, waiting for transfers between devices, local(): got = lax.all_to_all(sent, 'vec', split_axis=0, concat_axis=0, tiled=True)  6.93 us
    all_to_all x1, starting transfers between devices, local(): lax.all_to_all(back, 'vec', split_axis=0, concat_axis=0, tiled=True)  3.96 us
    pallas_call x1, Pallas kernels, prepare(): pl.pallas_call(prepare_kernel, out_shape=(pltpu.HBM((total // columns, gr...  2.68 us
  transfers between devices with their start and end apart: 16, of which 10 were waited for; matrix products, arithmetic and copies ran while one was open for 0% of the time, Pallas kernels for 13%

commit v1 on v0

--- a/solution.py
+++ b/solution.py
@@ -141,9 +141,10 @@
 def step_kernel(first, last, count, place, listing, held, low, high, *refs):
     parts, refs = list(refs[:PARTS]), list(refs[PARTS:])
     moved = refs.pop()
-    field = refs.pop()
     listed, rows = listing.shape
     chunk = rows // 2 // 4
+    operand = refs.pop() if last else None
+    field = refs.pop()
     if first:
         source, parts[-1] = parts[-1], refs.pop()
 
@@ -160,7 +161,7 @@
         current, previous = refs[:2]
         refs = refs[2:]
     if last:
-        result, operand = refs
+        (result,) = refs
 
         def store(index):
             some = pl.ds(index * 2 * chunk, 2 * chunk)
@@ -170,7 +171,9 @@
         operand = refs[0]
     columns, width = held.shape[1:]
     shift = place[0] * rows - HB
-    field[HB : HB + rows] = held[...]
+    base = 0 if last else HB
+    if first:
+        field[HB : HB + rows] = held[...]
     if count == 2:
         received = low[...]
         nothing = jnp.zeros_like(received)
@@ -191,7 +194,7 @@
                 2.0 * (product - centre * current[row]) / half_width
                 - previous[row].astype(jnp.float32)
             )
-        operand[row] = following.astype(jnp.bfloat16)
+        operand[base + row] = following.astype(jnp.bfloat16)
         if not last:
             refs[1][row] = following
 
@@ -222,16 +225,17 @@
         for index in range(4):
             store(index).wait()
     elif count == 2:
-        start = jnp.where(place[0] == 0, rows - HB, 0)
+        start = jnp.where(place[0] == 0, rows, HB)
         refs[2][...] = operand[pl.ds(start, HB)]
     else:
-        refs[2][...] = operand[:HB]
-        refs[3][...] = operand[rows - HB :]
+        refs[2][...] = operand[HB : 2 * HB]
+        refs[3][...] = operand[rows : rows + HB]
 
 
 def filter_step(turn, count, place, listing, held, halo, parts, state):
     first, last = turn == 0, turn == STEPS - 1
-    rows, columns, width = held.shape
+    columns, width = held.shape[1:]
+    rows = listing.shape[1]
     edge = jax.ShapeDtypeStruct((HB, columns, width), jnp.bfloat16)
     parts = list(parts)
     tail = parts[-1]
@@ -239,21 +243,24 @@
         parts[-1] = in_hbm(tail)
     args = [place, listing, held, *halo, *parts, *state]
     in_specs = [SMEM, SMEM] + [VMEM] * (len(args) - 2)
-    scratch = [pltpu.VMEM((rows + 2 * HB, columns, width), jnp.bfloat16)]
+    field = jax.ShapeDtypeStruct((rows + 2 * HB, columns, width), jnp.bfloat16)
+    scratch, aliases = [], {}
     if last:
-        out_shape = [pltpu.HBM(held.shape, jnp.bfloat16)]
+        out_shape = [pltpu.HBM((rows, columns, width), jnp.bfloat16)]
         out_specs = [ANY]
-        scratch = [pltpu.VMEM(held.shape, jnp.bfloat16)] + scratch
-    else:
-        out_shape = [
-            jax.ShapeDtypeStruct(held.shape, jnp.bfloat16),
-            jax.ShapeDtypeStruct(held.shape, jnp.float32),
-        ]
+        scratch = [pltpu.VMEM((rows, columns, width), jnp.bfloat16)]
+    else:
+        out_shape = [field, jax.ShapeDtypeStruct((rows, columns, width), jnp.float32)]
         out_shape += [edge] if count == 2 else [edge, edge]
         if first:
             in_specs[5 + PARTS - 1] = ANY
             out_shape.append(jax.ShapeDtypeStruct(tail.shape, tail.dtype))
+            scratch = [pltpu.VMEM(field.shape, field.dtype)]
         out_specs = [VMEM] * len(out_shape)
+    if not first:
+        aliases = {2: len(out_shape)}
+        out_shape.append(field)
+        out_specs.append(VMEM)
     scratch.append(pltpu.SemaphoreType.DMA((4,)))
     size = sum(part.size for part in parts)
     return pl.pallas_call(
@@ -261,6 +268,7 @@
         out_shape=out_shape,
         in_specs=in_specs,
         out_specs=out_specs,
+        input_output_aliases=aliases,
         scratch_shapes=scratch,
         compiler_params=pltpu.CompilerParams(vmem_limit_bytes=8 * 2**20),
         cost_estimate=pl.CostEstimate(

time: 87.8 us -> 87.8 us (level)
  no operation moved by 1% of the time
where the time goes in v1:
time: 87.8 us; the launch traced here: 87.3 us
  waiting for transfers between devices  37.3 us (42%)
  Pallas kernels  26.8 us (31%)
  starting transfers between devices  22.9 us (26%)
    ppermute x6, waiting for transfers between devices, meet(): return lax.ppermute(array, 'vec', pairs)  26.2 us
    pallas_call x4, Pallas kernels, filter_step(): pl.pallas_call(functools.partial(step_kernel, first, last, count), out_sh...  10.8 us
    pallas_call x2, Pallas kernels, turn_blocks(): pl.pallas_call(turn_kernel, grid=(rows // TURNED,), out_shape=space((rows...  10.3 us
    ppermute x6, starting transfers between devices, meet(): return lax.ppermute(array, 'vec', pairs)  8.75 us
    all_to_all x1, starting transfers between devices, local(): got = lax.all_to_all(sent, 'vec', split_axis=0, concat_axis=0, tiled=True)  8.36 us
    all_to_all x1, waiting for transfers between devices, local(): got = lax.all_to_all(sent, 'vec', split_axis=0, concat_axis=0, tiled=True)  6.94 us
    all_to_all x1, starting transfers between devices, local(): lax.all_to_all(back, 'vec', split_axis=0, concat_axis=0, tiled=True)  3.96 us
    pallas_call x1, Pallas kernels, prepare(): pl.pallas_call(prepare_kernel, out_shape=(pltpu.HBM((total // columns, gr...  2.68 us
  transfers between devices with their start and end apart: 16, of which 10 were waited for; matrix products, arithmetic and copies ran while one was open for 0% of the time, Pallas kernels for 13%

profile of v1, /device:TPU:0, one launch (start us, length us, event | category | flops | bytes accessed | tf_op | source)
XLA Modules:
  0.0 87.3 jit_solution(5871203696881583952)
XLA Ops:
  0.0 0.1 pad_add_fusion.place
  0.1 2.7 %prepare.1 = (bf16[16,2,64,128]{3,2,1,0:T(8,128)(2,1)}, bf16[1,32,1024]{2,1,0:T(8,128)(2,1)S(1)}) custom-call(s32[3]{0:T(128)S(1)} %pad_add_fusion.place, bf16[1,256,1024]{2,1,0:T(8,128)(2,1)} %vectors.1, bf16[64,1024]{1,0:T(8,128)(2,1)} %bitcast.16), custom_call_target="tpu_custom_call" | custom-call | tf_op jit(solution)/shard_map/prepare/pallas_call | solution.py:86
  2.8 8.4 %all-to-all-start = ((bf16[16,2,64,128]{3,2,1,0:T(8,128)(2,1)}), bf16[16,2,64,128]{3,2,1,0:T(8,128)(2,1)S(1)}, u32[]{:S(2)}, u32[]{:S(2)}) async-start(bf16[16,2,64,128]{3,2,1,0:T(8,128)(2,1)} %get-tuple-element.18), calls=%async_computation | async-start | bytes 1048576 | tf_op jit(solution)/shard_map/all_to_all | solution.py:409
  11.1 8.1 %turn_blocks.3.refs_1_ = bf16[12,1024,256]{2,1,0:T(8,128)(2,1)} custom-call(bf16[32,8,128,128]{3,2,1,0:T(8,128)(2,1)} %blocks.3), custom_call_target="tpu_custom_call" | custom-call | flops 1610612736 | bytes 12582912 | tf_op jit(solution)/shard_map/turn_blocks/pallas_call | solution.py:125
  19.3 6.9 %all-to-all-done = bf16[16,2,64,128]{3,2,1,0:T(8,128)(2,1)S(1)} async-done(((bf16[16,2,64,128]{3,2,1,0:T(8,128)(2,1)}), bf16[16,2,64,128]{3,2,1,0:T(8,128)(2,1)S(1)}, u32[]{:S(2)}, u32[]{:S(2)}) %all-to-all-start) | async-done | bytes 524320 | tf_op jit(solution)/shard_map/all_to_all | solution.py:409
  26.2 0.0 collective-permute-start
  26.2 2.2 %turn_blocks.2.refs_0_ = bf16[4,1024,256]{2,1,0:T(8,128)(2,1)S(1)} custom-call(bf16[32,8,128,128]{3,2,1,0:T(8,128)(2,1)} %blocks.3), custom_call_target="tpu_custom_call" | custom-call | flops 536870912 | bytes 4194304 | tf_op jit(solution)/shard_map/turn_blocks/pallas_call | solution.py:125
  28.4 4.0 %filter_step.4 = (bf16[36,64,128]{2,1,0:T(8,128)(2,1)S(1)}, f32[32,64,128]{2,1,0:T(8,128)S(1)}, bf16[2,64,128]{2,1,0:T(8,128)(2,1)S(1)}, bf16[12,1024,256]{2,1,0:T(8,128)(2,1)S(1)}) custom-call(s32[3]{0:T(128)S(1)} %pad_add_fusion.place, s32[8,32]{1,0:T(8,128)S(1)} %bitcast.11, bf16[32,64,128]{2,1,0:T(8,128)(2,1)S(1)} %bitcast.9, ...), custom_call_target="tpu_custom_call" | custom-call | flops 536870912 | bytes 8388608 | tf_op jit(solution)/shard_map/filter_step/pallas_call | solution.py:266
  32.4 0.6 collective-permute-start.1
  33.0 0.9 collective-permute-done.1.low.high
  33.8 2.1 %filter_step.5 = (bf16[36,64,128]{2,1,0:T(8,128)(2,1)S(1)}, f32[32,64,128]{2,1,0:T(8,128)S(1)}, bf16[2,64,128]{2,1,0:T(8,128)(2,1)S(1)}, bf16[36,64,128]{2,1,0:T(8,128)(2,1)S(1)}) custom-call(s32[3]{0:T(128)S(1)} %pad_add_fusion.place, s32[8,32]{1,0:T(8,128)S(1)} %bitcast.12, ...), custom_call_target="tpu_custom_call", output_to_operand_aliasing={{3}: (2, {})} | custom-call | flops 536870912 | bytes 8388608 | tf_op jit(solution)/shard_map/filter_step/pallas_call | solution.py:266
  35.9 0.4 collective-permute-start.2
  36.3 0.9 %collective-permute-done.2.low.high = bf16[2,64,128]{2,1,0:T(8,128)(2,1)S(1)} collective-permute-done((bf16[2,64,128]{2,1,0:T(8,128)(2,1)S(1)}, bf16[2,64,128]{2,1,0:T(8,128)(2,1)S(1)}, u32[]{:S(2)}, u32[]{:S(2)}) %collective-permute-start.2) | collective-permute-done | bytes 32800 | tf_op jit(solution)/shard_map/ppermute | solution.py:300
  37.2 2.1 %filter_step.6 = (bf16[36,64,128]{2,1,0:T(8,128)(2,1)S(1)}, f32[32,64,128]{2,1,0:T(8,128)S(1)}, bf16[2,64,128]{2,1,0:T(8,128)(2,1)S(1)}, bf16[36,64,128]{2,1,0:T(8,128)(2,1)S(1)}) custom-call(s32[3]{0:T(128)S(1)} %pad_add_fusion.place, s32[8,32]{1,0:T(8,128)S(1)} %bitcast.13, ...), custom_call_target="tpu_custom_call", output_to_operand_aliasing={{3}: (2, {})} | custom-call | flops 536870912 | bytes 8388608 | tf_op jit(solution)/shard_map/filter_step/pallas_call | solution.py:266
  39.3 0.4 collective-permute-start.3
  39.6 0.9 %collective-permute-done.3.low.high = bf16[2,64,128]{2,1,0:T(8,128)(2,1)S(1)} collective-permute-done((bf16[2,64,128]{2,1,0:T(8,128)(2,1)S(1)}, bf16[2,64,128]{2,1,0:T(8,128)(2,1)S(1)}, u32[]{:S(2)}, u32[]{:S(2)}) %collective-permute-start.3) | collective-permute-done | bytes 32800 | tf_op jit(solution)/shard_map/ppermute | solution.py:300
  40.5 2.7 %filter_step.7 = (bf16[32,64,128]{2,1,0:T(8,128)(2,1)}, bf16[36,64,128]{2,1,0:T(8,128)(2,1)S(1)}) custom-call(s32[3]{0:T(128)S(1)} %pad_add_fusion.place, s32[8,32]{1,0:T(8,128)S(1)} %bitcast.14, bf16[36,64,128]{2,1,0:T(8,128)(2,1)S(1)} %get-tuple-element.26.held, ...), custom_call_target="tpu_custom_call", output_to_operand_aliasing={{1}: (2, {})} | custom-call | flops 536870912 | bytes 8388608 | tf_op jit(solution)/shard_map/filter_step/pallas_call | solution.py:266
  43.2 4.0 %all-to-all-start.1 = ((bf16[16,2,64,128]{3,2,1,0:T(8,128)(2,1)}), bf16[16,2,64,128]{3,2,1,0:T(8,128)(2,1)S(1)}, u32[]{:S(2)}, u32[]{:S(2)}) async-start(bf16[16,2,64,128]{3,2,1,0:T(8,128)(2,1)} %bitcast.15), calls=%async_computation.1 | async-start | bytes 1048576 | tf_op jit(solution)/shard_map/all_to_all | solution.py:448
  47.2 2.8 %collective-permute-start.5 = (bf16[1,32,1024]{2,1,0:T(8,128)(2,1)S(1)}, bf16[1,32,1024]{2,1,0:T(8,128)(2,1)S(1)}, u32[]{:S(2)}, u32[]{:S(2)}) collective-permute-start(bf16[1,32,1024]{2,1,0:T(8,128)(2,1)S(1)} %get-tuple-element.30.refs_0_), channel_id=1, source_target_pairs={{0,16},{2,18},{4,20},{6,22},{8,24},{10,26},{12,28},{14,30},{16,0},... | collective-permute-start | bytes 196616 | tf_op jit(solution)/shard_map/ppermute | solution.py:310
  50.0 1.5 %collective-permute-start.4 = (bf16[1,32,1024]{2,1,0:T(8,128)(2,1)S(1)}, bf16[1,32,1024]{2,1,0:T(8,128)(2,1)S(1)}, u32[]{:S(2)}, u32[]{:S(2)}) collective-permute-start(bf16[1,32,1024]{2,1,0:T(8,128)(2,1)S(1)} %get-tuple-element.30.refs_0_), channel_id=1, source_target_pairs={{0,8},{2,10},{4,12},{6,14},{8,0},{10,2},{12,4},{14,6},{16,24},{18,... | collective-permute-start | bytes 196616 | tf_op jit(solution)/shard_map/ppermute | solution.py:310
  51.5 13.4 %collective-permute-done.5.refs_2_ = bf16[1,32,1024]{2,1,0:T(8,128)(2,1)S(1)} collective-permute-done((bf16[1,32,1024]{2,1,0:T(8,128)(2,1)S(1)}, bf16[1,32,1024]{2,1,0:T(8,128)(2,1)S(1)}, u32[]{:S(2)}, u32[]{:S(2)}) %collective-permute-start.5) | collective-permute-done | bytes 65568 | tf_op jit(solution)/shard_map/ppermute | solution.py:310
  64.9 4.3 %collective-permute-done.6.refs_3_ = bf16[1,32,1024]{2,1,0:T(8,128)(2,1)S(1)} collective-permute-done((bf16[1,32,1024]{2,1,0:T(8,128)(2,1)S(1)}, bf16[1,32,1024]{2,1,0:T(8,128)(2,1)S(1)}, u32[]{:S(2)}, u32[]{:S(2)}) %collective-permute-start.6) | collective-permute-done | bytes 65568 | tf_op jit(solution)/shard_map/ppermute | solution.py:310
  69.2 1.5 %collective-permute-start.7 = (bf16[4,32,1024]{2,1,0:T(8,128)(2,1)S(1)}, bf16[4,32,1024]{2,1,0:T(8,128)(2,1)S(1)}, u32[]{:S(2)}, u32[]{:S(2)}) collective-permute-start(bf16[4,32,1024]{2,1,0:T(8,128)(2,1)S(1)} %join.1.refs_0_), channel_id=1, source_target_pairs={{0,2},{2,0},{4,6},{6,4},{8,10},{10,8},{12,14},{14,12},{16,18},{18,... | collective-permute-start | bytes 786440 | tf_op jit(solution)/shard_map/ppermute | solution.py:310
  70.7 1.5 %collective-permute-start.8 = (bf16[4,32,1024]{2,1,0:T(8,128)(2,1)S(1)}, bf16[4,32,1024]{2,1,0:T(8,128)(2,1)S(1)}, u32[]{:S(2)}, u32[]{:S(2)}) collective-permute-start(bf16[4,32,1024]{2,1,0:T(8,128)(2,1)S(1)} %join.1.refs_0_), channel_id=1, source_target_pairs={{0,4},{2,6},{4,0},{6,2},{8,12},{10,14},{12,8},{14,10},{16,20},{18,... | collective-permute-start | bytes 786440 | tf_op jit(solution)/shard_map/ppermute | solution.py:310
  72.1 3.4 %collective-permute-done.7.refs_1_ = bf16[4,32,1024]{2,1,0:T(8,128)(2,1)S(1)} collective-permute-done((bf16[4,32,1024]{2,1,0:T(8,128)(2,1)S(1)}, bf16[4,32,1024]{2,1,0:T(8,128)(2,1)S(1)}, u32[]{:S(2)}, u32[]{:S(2)}) %collective-permute-start.7) | collective-permute-done | bytes 262176 | tf_op jit(solution)/shard_map/ppermute | solution.py:310
  75.6 1.5 %collective-permute-start.9 = (bf16[4,32,1024]{2,1,0:T(8,128)(2,1)S(1)}, bf16[4,32,1024]{2,1,0:T(8,128)(2,1)S(1)}, u32[]{:S(2)}, u32[]{:S(2)}) collective-permute-start(bf16[4,32,1024]{2,1,0:T(8,128)(2,1)S(1)} %collective-permute-done.7.refs_1_), channel_id=1, source_target_pairs={{0,4},{2,6},{4,0},{6,2},{8,12},{10,14},{12,8},{14,10},{16,20},{18,... | collective-permute-start | bytes 786440 | tf_op jit(solution)/shard_map/ppermute | solution.py:310
  77.1 0.5 collective-permute-start.11
  77.6 1.6 %collective-permute-done.8.refs_2_ = bf16[4,32,1024]{2,1,0:T(8,128)(2,1)S(1)} collective-permute-done((bf16[4,32,1024]{2,1,0:T(8,128)(2,1)S(1)}, bf16[4,32,1024]{2,1,0:T(8,128)(2,1)S(1)}, u32[]{:S(2)}, u32[]{:S(2)}) %collective-permute-start.8) | collective-permute-done | bytes 262176 | tf_op jit(solution)/shard_map/ppermute | solution.py:310
  79.2 3.5 %collective-permute-done.9.refs_3_ = bf16[4,32,1024]{2,1,0:T(8,128)(2,1)S(1)} collective-permute-done((bf16[4,32,1024]{2,1,0:T(8,128)(2,1)S(1)}, bf16[4,32,1024]{2,1,0:T(8,128)(2,1)S(1)}, u32[]{:S(2)}, u32[]{:S(2)}) %collective-permute-start.9) | collective-permute-done | bytes 262176 | tf_op jit(solution)/shard_map/ppermute | solution.py:310
  82.7 1.5 %collective-permute-done.13.refs_7_ = bf16[4,32,1024]{2,1,0:T(8,128)(2,1)S(1)} collective-permute-done((bf16[4,32,1024]{2,1,0:T(8,128)(2,1)S(1)}, bf16[4,32,1024]{2,1,0:T(8,128)(2,1)S(1)}, u32[]{:S(2)}, u32[]{:S(2)}) %collective-permute-start.13) | collective-permute-done | bytes 262176 | tf_op jit(solution)/shard_map/ppermute | solution.py:451
  84.2 1.4 %assemble.1.rotation = bf16[1024,1024]{1,0:T(8,128)(2,1)S(1)} custom-call(s32[3]{0:T(128)S(1)} %pad_add_fusion.place, bf16[4,32,1024]{2,1,0:T(8,128)(2,1)S(1)} %join.1.refs_0_, bf16[4,32,1024]{2,1,0:T(8,128)(2,1)S(1)} %collective-permute-done.7.refs_1_, bf16[4,32,1024]{2,1,0:T(8,128)(2,1)S(1)} %collective-permute-done.8.refs_2_, ...), custom_call_target="tpu_custom_call" | custom-call | flops 536870912 | bytes 4194304 | tf_op jit(solution)/shard_map/assemble/pallas_call | solution.py:338
  85.7 1.6 %rotate.1 = bf16[256,1024]{1,0:T(8,128)(2,1)} custom-call(bf16[16,2,64,128]{3,2,1,0:T(8,128)(2,1)S(1)} %all-to-all-done.1.filtered, bf16[1024,1024]{1,0:T(8,128)(2,1)S(1)} %assemble.1.rotation), custom_call_target="tpu_custom_call" | custom-call | tf_op jit(solution)/shard_map/rotate/pallas_call | solution.py:379
  (14 shorter events, 0.1 us)
Async XLA Ops:
  2.8 23.4 %all-to-all-start = ((bf16[16,2,64,128]{3,2,1,0:T(8,128)(2,1)}), bf16[16,2,64,128]{3,2,1,0:T(8,128)(2,1)S(1)}, u32[]{:S(2)}, u32[]{:S(2)}) async-start(bf16[16,2,64,128]{3,2,1,0:T(8,128)(2,1)} %get-tuple-element.18), calls=%async_computation | async-start | bytes 1048576 | tf_op jit(solution)/shard_map/all_to_all | solution.py:409
  19.3 9.2 %copy-start = (s32[32,8]{0,1:T(8,128)S(1)}, s32[32,8]{0,1:T(8,128)}, u32[]{:S(2)}) copy-start(s32[32,8]{0,1:T(8,128)} %param.7) | copy-start | bytes 3076
  26.2 2.2 %collective-permute-start = (bf16[2,64,128]{2,1,0:T(8,128)(2,1)S(1)}, bf16[2,64,128]{2,1,0:T(8,128)(2,1)S(1)}, u32[]{:S(2)}, u32[]{:S(2)}) collective-permute-start(bf16[2,64,128]{2,1,0:T(8,128)(2,1)S(1)} %constant_dynamic-slice_fusion.refs_4_), channel_id=1, source_target_pairs={{0,1},{1,0},{2,3},{3,2},{4,5},{5,4},{6,7},{7,6},{8,9},{9,8},{10,11... | collective-permute-start | bytes 98312 | tf_op jit(solution)/shard_map/ppermute | solution.py:300
  32.4 1.4 %collective-permute-start.1 = (bf16[2,64,128]{2,1,0:T(8,128)(2,1)S(1)}, bf16[2,64,128]{2,1,0:T(8,128)(2,1)S(1)}, u32[]{:S(2)}, u32[]{:S(2)}) collective-permute-start(bf16[2,64,128]{2,1,0:T(8,128)(2,1)S(1)} %get-tuple-element.20), channel_id=1, source_target_pairs={{0,1},{1,0},{2,3},{3,2},{4,5},{5,4},{6,7},{7,6},{8,9},{9,8},{10,11... | collective-permute-start | bytes 98312 | tf_op jit(solution)/shard_map/ppermute | solution.py:300
  35.9 1.3 %collective-permute-start.2 = (bf16[2,64,128]{2,1,0:T(8,128)(2,1)S(1)}, bf16[2,64,128]{2,1,0:T(8,128)(2,1)S(1)}, u32[]{:S(2)}, u32[]{:S(2)}) collective-permute-start(bf16[2,64,128]{2,1,0:T(8,128)(2,1)S(1)} %get-tuple-element.24), channel_id=1, source_target_pairs={{0,1},{1,0},{2,3},{3,2},{4,5},{5,4},{6,7},{7,6},{8,9},{9,8},{10,11... | collective-permute-start | bytes 98312 | tf_op jit(solution)/shard_map/ppermute | solution.py:300
  39.3 1.3 %collective-permute-start.3 = (bf16[2,64,128]{2,1,0:T(8,128)(2,1)S(1)}, bf16[2,64,128]{2,1,0:T(8,128)(2,1)S(1)}, u32[]{:S(2)}, u32[]{:S(2)}) collective-permute-start(bf16[2,64,128]{2,1,0:T(8,128)(2,1)S(1)} %get-tuple-element.27), channel_id=1, source_target_pairs={{0,1},{1,0},{2,3},{3,2},{4,5},{5,4},{6,7},{7,6},{8,9},{9,8},{10,11... | collective-permute-start | bytes 98312 | tf_op jit(solution)/shard_map/ppermute | solution.py:300
  43.2 42.4 %all-to-all-start.1 = ((bf16[16,2,64,128]{3,2,1,0:T(8,128)(2,1)}), bf16[16,2,64,128]{3,2,1,0:T(8,128)(2,1)S(1)}, u32[]{:S(2)}, u32[]{:S(2)}) async-start(bf16[16,2,64,128]{3,2,1,0:T(8,128)(2,1)} %bitcast.15), calls=%async_computation.1 | async-start | bytes 1048576 | tf_op jit(solution)/shard_map/all_to_all | solution.py:448
  47.2 17.7 %collective-permute-start.5 = (bf16[1,32,1024]{2,1,0:T(8,128)(2,1)S(1)}, bf16[1,32,1024]{2,1,0:T(8,128)(2,1)S(1)}, u32[]{:S(2)}, u32[]{:S(2)}) collective-permute-start(bf16[1,32,1024]{2,1,0:T(8,128)(2,1)S(1)} %get-tuple-element.30.refs_0_), channel_id=1, source_target_pairs={{0,16},{2,18},{4,20},{6,22},{8,24},{10,26},{12,28},{14,30},{16,0},... | collective-permute-start | bytes 196616 | tf_op jit(solution)/shard_map/ppermute | solution.py:310
  50.0 14.9 %collective-permute-start.4 = (bf16[1,32,1024]{2,1,0:T(8,128)(2,1)S(1)}, bf16[1,32,1024]{2,1,0:T(8,128)(2,1)S(1)}, u32[]{:S(2)}, u32[]{:S(2)}) collective-permute-start(bf16[1,32,1024]{2,1,0:T(8,128)(2,1)S(1)} %get-tuple-element.30.refs_0_), channel_id=1, source_target_pairs={{0,8},{2,10},{4,12},{6,14},{8,0},{10,2},{12,4},{14,6},{16,24},{18,... | collective-permute-start | bytes 196616 | tf_op jit(solution)/shard_map/ppermute | solution.py:310
  64.9 4.3 %collective-permute-start.6 = (bf16[1,32,1024]{2,1,0:T(8,128)(2,1)S(1)}, bf16[1,32,1024]{2,1,0:T(8,128)(2,1)S(1)}, u32[]{:S(2)}, u32[]{:S(2)}) collective-permute-start(bf16[1,32,1024]{2,1,0:T(8,128)(2,1)S(1)} %collective-permute-done.5.refs_2_), channel_id=1, source_target_pairs={{0,8},{2,10},{4,12},{6,14},{8,0},{10,2},{12,4},{14,6},{16,24},{18,... | collective-permute-start | bytes 196616 | tf_op jit(solution)/shard_map/ppermute | solution.py:310
  69.2 6.4 %collective-permute-start.7 = (bf16[4,32,1024]{2,1,0:T(8,128)(2,1)S(1)}, bf16[4,32,1024]{2,1,0:T(8,128)(2,1)S(1)}, u32[]{:S(2)}, u32[]{:S(2)}) collective-permute-start(bf16[4,32,1024]{2,1,0:T(8,128)(2,1)S(1)} %join.1.refs_0_), channel_id=1, source_target_pairs={{0,2},{2,0},{4,6},{6,4},{8,10},{10,8},{12,14},{14,12},{16,18},{18,... | collective-permute-start | bytes 786440 | tf_op jit(solution)/shard_map/ppermute | solution.py:310
  70.7 8.5 %collective-permute-start.8 = (bf16[4,32,1024]{2,1,0:T(8,128)(2,1)S(1)}, bf16[4,32,1024]{2,1,0:T(8,128)(2,1)S(1)}, u32[]{:S(2)}, u32[]{:S(2)}) collective-permute-start(bf16[4,32,1024]{2,1,0:T(8,128)(2,1)S(1)} %join.1.refs_0_), channel_id=1, source_target_pairs={{0,4},{2,6},{4,0},{6,2},{8,12},{10,14},{12,8},{14,10},{16,20},{18,... | collective-permute-start | bytes 786440 | tf_op jit(solution)/shard_map/ppermute | solution.py:310
  75.6 7.1 %collective-permute-start.9 = (bf16[4,32,1024]{2,1,0:T(8,128)(2,1)S(1)}, bf16[4,32,1024]{2,1,0:T(8,128)(2,1)S(1)}, u32[]{:S(2)}, u32[]{:S(2)}) collective-permute-start(bf16[4,32,1024]{2,1,0:T(8,128)(2,1)S(1)} %collective-permute-done.7.refs_1_), channel_id=1, source_target_pairs={{0,4},{2,6},{4,0},{6,2},{8,12},{10,14},{12,8},{14,10},{16,20},{18,... | collective-permute-start | bytes 786440 | tf_op jit(solution)/shard_map/ppermute | solution.py:310
  77.1 5.6 %collective-permute-start.10 = (bf16[4,32,1024]{2,1,0:T(8,128)(2,1)S(1)}, bf16[4,32,1024]{2,1,0:T(8,128)(2,1)S(1)}, u32[]{:S(2)}, u32[]{:S(2)}) collective-permute-start(bf16[4,32,1024]{2,1,0:T(8,128)(2,1)S(1)} %join.1.refs_0_), channel_id=1, source_target_pairs={{0,1},{1,0},{2,3},{3,2},{4,5},{5,4},{6,7},{7,6},{8,9},{9,8},{10,11... | collective-permute-start | bytes 786440 | tf_op jit(solution)/shard_map/ppermute | solution.py:451
  77.1 5.6 %collective-permute-start.11 = (bf16[4,32,1024]{2,1,0:T(8,128)(2,1)S(1)}, bf16[4,32,1024]{2,1,0:T(8,128)(2,1)S(1)}, u32[]{:S(2)}, u32[]{:S(2)}) collective-permute-start(bf16[4,32,1024]{2,1,0:T(8,128)(2,1)S(1)} %collective-permute-done.7.refs_1_), channel_id=1, source_target_pairs={{0,1},{1,0},{2,3},{3,2},{4,5},{5,4},{6,7},{7,6},{8,9},{9,8},{10,11... | collective-permute-start | bytes 786440 | tf_op jit(solution)/shard_map/ppermute | solution.py:451
  79.2 3.5 %collective-permute-start.12 = (bf16[4,32,1024]{2,1,0:T(8,128)(2,1)S(1)}, bf16[4,32,1024]{2,1,0:T(8,128)(2,1)S(1)}, u32[]{:S(2)}, u32[]{:S(2)}) collective-permute-start(bf16[4,32,1024]{2,1,0:T(8,128)(2,1)S(1)} %collective-permute-done.8.refs_2_), channel_id=1, source_target_pairs={{0,1},{1,0},{2,3},{3,2},{4,5},{5,4},{6,7},{7,6},{8,9},{9,8},{10,11... | collective-permute-start | bytes 786440 | tf_op jit(solution)/shard_map/ppermute | solution.py:451
  82.7 1.5 %collective-permute-start.13 = (bf16[4,32,1024]{2,1,0:T(8,128)(2,1)S(1)}, bf16[4,32,1024]{2,1,0:T(8,128)(2,1)S(1)}, u32[]{:S(2)}, u32[]{:S(2)}) collective-permute-start(bf16[4,32,1024]{2,1,0:T(8,128)(2,1)S(1)} %collective-permute-done.9.refs_3_), channel_id=1, source_target_pairs={{0,1},{1,0},{2,3},{3,2},{4,5},{5,4},{6,7},{7,6},{8,9},{9,8},{10,11... | collective-permute-start | bytes 786440 | tf_op jit(solution)/shard_map/ppermute | solution.py:451

commit v2 on v1

--- a/solution.py
+++ b/solution.py
@@ -11,8 +11,8 @@
 HB = 2
 STEPS = 4
 PARTS = 2
-LOADS = 3
-TURNED = 4
+LOADS = 6
+TURNED = 8
 DIRECT = 2
 
 centre = 0.3
@@ -261,7 +261,7 @@
         aliases = {2: len(out_shape)}
         out_shape.append(field)
         out_specs.append(VMEM)
-    scratch.append(pltpu.SemaphoreType.DMA((4,)))
+    scratch.append(pltpu.SemaphoreType.DMA((8,)))
     size = sum(part.size for part in parts)
     return pl.pallas_call(
         functools.partial(step_kernel, first, last, count),

time: 87.8 us -> 87.8 us (level)
  no operation moved by 1% of the time
where the time goes in v2:
time: 87.8 us; the launch traced here: 87.3 us
  waiting for transfers between devices  37.9 us (43%)
  Pallas kernels  26.3 us (30%)
  starting transfers between devices  22.9 us (26%)
    ppermute x6, waiting for transfers between devices, meet(): return lax.ppermute(array, 'vec', pairs)  26.2 us
    pallas_call x4, Pallas kernels, filter_step(): pl.pallas_call(functools.partial(step_kernel, first, last, count), out_sh...  10.7 us
    pallas_call x2, Pallas kernels, turn_blocks(): pl.pallas_call(turn_kernel, grid=(rows // TURNED,), out_shape=space((rows...  9.89 us
    ppermute x6, starting transfers between devices, meet(): return lax.ppermute(array, 'vec', pairs)  8.75 us
    all_to_all x1, starting transfers between devices, local(): got = lax.all_to_all(sent, 'vec', split_axis=0, concat_axis=0, tiled=True)  8.36 us
    all_to_all x1, waiting for transfers between devices, local(): got = lax.all_to_all(sent, 'vec', split_axis=0, concat_axis=0, tiled=True)  7.51 us
    all_to_all x1, starting transfers between devices, local(): lax.all_to_all(back, 'vec', split_axis=0, concat_axis=0, tiled=True)  3.96 us
    pallas_call x1, Pallas kernels, prepare(): pl.pallas_call(prepare_kernel, out_shape=(pltpu.HBM((total // columns, gr...  2.68 us
  transfers between devices with their start and end apart: 16, of which 10 were waited for; matrix products, arithmetic and copies ran while one was open for 0% of the time, Pallas kernels for 13%

profile of v2, /device:TPU:0, one launch (start us, length us, event | category | flops | bytes accessed | tf_op | source)
XLA Modules:
  0.0 87.3 jit_solution(16485959603734207999)
XLA Ops:
  0.0 0.1 pad_add_fusion.place
  0.1 2.7 %prepare.1 = (bf16[16,2,64,128]{3,2,1,0:T(8,128)(2,1)}, bf16[1,32,1024]{2,1,0:T(8,128)(2,1)S(1)}) custom-call(s32[3]{0:T(128)S(1)} %pad_add_fusion.place, bf16[1,256,1024]{2,1,0:T(8,128)(2,1)} %vectors.1, bf16[64,1024]{1,0:T(8,128)(2,1)} %bitcast.16), custom_call_target="tpu_custom_call" | custom-call | tf_op jit(solution)/shard_map/prepare/pallas_call | solution.py:86
  2.8 8.4 %all-to-all-start = ((bf16[16,2,64,128]{3,2,1,0:T(8,128)(2,1)}), bf16[16,2,64,128]{3,2,1,0:T(8,128)(2,1)S(1)}, u32[]{:S(2)}, u32[]{:S(2)}) async-start(bf16[16,2,64,128]{3,2,1,0:T(8,128)(2,1)} %get-tuple-element.18), calls=%async_computation | async-start | bytes 1048576 | tf_op jit(solution)/shard_map/all_to_all | solution.py:409
  11.1 7.6 %turn_blocks.3.refs_1_ = bf16[12,1024,256]{2,1,0:T(8,128)(2,1)} custom-call(bf16[32,8,128,128]{3,2,1,0:T(8,128)(2,1)} %blocks.3), custom_call_target="tpu_custom_call" | custom-call | flops 1610612736 | bytes 12582912 | tf_op jit(solution)/shard_map/turn_blocks/pallas_call | solution.py:125
  18.7 7.5 %all-to-all-done = bf16[16,2,64,128]{3,2,1,0:T(8,128)(2,1)S(1)} async-done(((bf16[16,2,64,128]{3,2,1,0:T(8,128)(2,1)}), bf16[16,2,64,128]{3,2,1,0:T(8,128)(2,1)S(1)}, u32[]{:S(2)}, u32[]{:S(2)}) %all-to-all-start) | async-done | bytes 524320 | tf_op jit(solution)/shard_map/all_to_all | solution.py:409
  26.2 0.0 collective-permute-start
  26.2 2.3 %turn_blocks.2.refs_0_ = bf16[4,1024,256]{2,1,0:T(8,128)(2,1)S(1)} custom-call(bf16[32,8,128,128]{3,2,1,0:T(8,128)(2,1)} %blocks.3), custom_call_target="tpu_custom_call" | custom-call | flops 536870912 | bytes 4194304 | tf_op jit(solution)/shard_map/turn_blocks/pallas_call | solution.py:125
  28.6 3.8 %filter_step.4 = (bf16[36,64,128]{2,1,0:T(8,128)(2,1)S(1)}, f32[32,64,128]{2,1,0:T(8,128)S(1)}, bf16[2,64,128]{2,1,0:T(8,128)(2,1)S(1)}, bf16[12,1024,256]{2,1,0:T(8,128)(2,1)S(1)}) custom-call(s32[3]{0:T(128)S(1)} %pad_add_fusion.place, s32[8,32]{1,0:T(8,128)S(1)} %bitcast.11, bf16[32,64,128]{2,1,0:T(8,128)(2,1)S(1)} %bitcast.9, ...), custom_call_target="tpu_custom_call" | custom-call | flops 536870912 | bytes 8388608 | tf_op jit(solution)/shard_map/filter_step/pallas_call | solution.py:266
  32.4 0.6 collective-permute-start.1
  32.9 0.9 collective-permute-done.1.low.high
  33.8 2.1 %filter_step.5 = (bf16[36,64,128]{2,1,0:T(8,128)(2,1)S(1)}, f32[32,64,128]{2,1,0:T(8,128)S(1)}, bf16[2,64,128]{2,1,0:T(8,128)(2,1)S(1)}, bf16[36,64,128]{2,1,0:T(8,128)(2,1)S(1)}) custom-call(s32[3]{0:T(128)S(1)} %pad_add_fusion.place, s32[8,32]{1,0:T(8,128)S(1)} %bitcast.12, ...), custom_call_target="tpu_custom_call", output_to_operand_aliasing={{3}: (2, {})} | custom-call | flops 536870912 | bytes 8388608 | tf_op jit(solution)/shard_map/filter_step/pallas_call | solution.py:266
  35.9 0.4 collective-permute-start.2
  36.3 0.9 %collective-permute-done.2.low.high = bf16[2,64,128]{2,1,0:T(8,128)(2,1)S(1)} collective-permute-done((bf16[2,64,128]{2,1,0:T(8,128)(2,1)S(1)}, bf16[2,64,128]{2,1,0:T(8,128)(2,1)S(1)}, u32[]{:S(2)}, u32[]{:S(2)}) %collective-permute-start.2) | collective-permute-done | bytes 32800 | tf_op jit(solution)/shard_map/ppermute | solution.py:300
  37.2 2.1 %filter_step.6 = (bf16[36,64,128]{2,1,0:T(8,128)(2,1)S(1)}, f32[32,64,128]{2,1,0:T(8,128)S(1)}, bf16[2,64,128]{2,1,0:T(8,128)(2,1)S(1)}, bf16[36,64,128]{2,1,0:T(8,128)(2,1)S(1)}) custom-call(s32[3]{0:T(128)S(1)} %pad_add_fusion.place, s32[8,32]{1,0:T(8,128)S(1)} %bitcast.13, ...), custom_call_target="tpu_custom_call", output_to_operand_aliasing={{3}: (2, {})} | custom-call | flops 536870912 | bytes 8388608 | tf_op jit(solution)/shard_map/filter_step/pallas_call | solution.py:266
  39.3 0.4 collective-permute-start.3
  39.7 0.9 %collective-permute-done.3.low.high = bf16[2,64,128]{2,1,0:T(8,128)(2,1)S(1)} collective-permute-done((bf16[2,64,128]{2,1,0:T(8,128)(2,1)S(1)}, bf16[2,64,128]{2,1,0:T(8,128)(2,1)S(1)}, u32[]{:S(2)}, u32[]{:S(2)}) %collective-permute-start.3) | collective-permute-done | bytes 32800 | tf_op jit(solution)/shard_map/ppermute | solution.py:300
  40.5 2.7 %filter_step.7 = (bf16[32,64,128]{2,1,0:T(8,128)(2,1)}, bf16[36,64,128]{2,1,0:T(8,128)(2,1)S(1)}) custom-call(s32[3]{0:T(128)S(1)} %pad_add_fusion.place, s32[8,32]{1,0:T(8,128)S(1)} %bitcast.14, bf16[36,64,128]{2,1,0:T(8,128)(2,1)S(1)} %get-tuple-element.26.held, ...), custom_call_target="tpu_custom_call", output_to_operand_aliasing={{1}: (2, {})} | custom-call | flops 536870912 | bytes 8388608 | tf_op jit(solution)/shard_map/filter_step/pallas_call | solution.py:266
  43.3 4.0 %all-to-all-start.1 = ((bf16[16,2,64,128]{3,2,1,0:T(8,128)(2,1)}), bf16[16,2,64,128]{3,2,1,0:T(8,128)(2,1)S(1)}, u32[]{:S(2)}, u32[]{:S(2)}) async-start(bf16[16,2,64,128]{3,2,1,0:T(8,128)(2,1)} %bitcast.15), calls=%async_computation.1 | async-start | bytes 1048576 | tf_op jit(solution)/shard_map/all_to_all | solution.py:448
  47.3 2.8 %collective-permute-start.5 = (bf16[1,32,1024]{2,1,0:T(8,128)(2,1)S(1)}, bf16[1,32,1024]{2,1,0:T(8,128)(2,1)S(1)}, u32[]{:S(2)}, u32[]{:S(2)}) collective-permute-start(bf16[1,32,1024]{2,1,0:T(8,128)(2,1)S(1)} %get-tuple-element.30.refs_0_), channel_id=1, source_target_pairs={{0,16},{2,18},{4,20},{6,22},{8,24},{10,26},{12,28},{14,30},{16,0},... | collective-permute-start | bytes 196616 | tf_op jit(solution)/shard_map/ppermute | solution.py:310
  50.1 1.5 %collective-permute-start.4 = (bf16[1,32,1024]{2,1,0:T(8,128)(2,1)S(1)}, bf16[1,32,1024]{2,1,0:T(8,128)(2,1)S(1)}, u32[]{:S(2)}, u32[]{:S(2)}) collective-permute-start(bf16[1,32,1024]{2,1,0:T(8,128)(2,1)S(1)} %get-tuple-element.30.refs_0_), channel_id=1, source_target_pairs={{0,8},{2,10},{4,12},{6,14},{8,0},{10,2},{12,4},{14,6},{16,24},{18,... | collective-permute-start | bytes 196616 | tf_op jit(solution)/shard_map/ppermute | solution.py:310
  51.6 13.4 %collective-permute-done.5.refs_2_ = bf16[1,32,1024]{2,1,0:T(8,128)(2,1)S(1)} collective-permute-done((bf16[1,32,1024]{2,1,0:T(8,128)(2,1)S(1)}, bf16[1,32,1024]{2,1,0:T(8,128)(2,1)S(1)}, u32[]{:S(2)}, u32[]{:S(2)}) %collective-permute-start.5) | collective-permute-done | bytes 65568 | tf_op jit(solution)/shard_map/ppermute | solution.py:310
  64.9 4.3 %collective-permute-done.6.refs_3_ = bf16[1,32,1024]{2,1,0:T(8,128)(2,1)S(1)} collective-permute-done((bf16[1,32,1024]{2,1,0:T(8,128)(2,1)S(1)}, bf16[1,32,1024]{2,1,0:T(8,128)(2,1)S(1)}, u32[]{:S(2)}, u32[]{:S(2)}) %collective-permute-start.6) | collective-permute-done | bytes 65568 | tf_op jit(solution)/shard_map/ppermute | solution.py:310
  69.2 1.5 %collective-permute-start.7 = (bf16[4,32,1024]{2,1,0:T(8,128)(2,1)S(1)}, bf16[4,32,1024]{2,1,0:T(8,128)(2,1)S(1)}, u32[]{:S(2)}, u32[]{:S(2)}) collective-permute-start(bf16[4,32,1024]{2,1,0:T(8,128)(2,1)S(1)} %join.1.refs_0_), channel_id=1, source_target_pairs={{0,2},{2,0},{4,6},{6,4},{8,10},{10,8},{12,14},{14,12},{16,18},{18,... | collective-permute-start | bytes 786440 | tf_op jit(solution)/shard_map/ppermute | solution.py:310
  70.8 1.5 %collective-permute-start.8 = (bf16[4,32,1024]{2,1,0:T(8,128)(2,1)S(1)}, bf16[4,32,1024]{2,1,0:T(8,128)(2,1)S(1)}, u32[]{:S(2)}, u32[]{:S(2)}) collective-permute-start(bf16[4,32,1024]{2,1,0:T(8,128)(2,1)S(1)} %join.1.refs_0_), channel_id=1, source_target_pairs={{0,4},{2,6},{4,0},{6,2},{8,12},{10,14},{12,8},{14,10},{16,20},{18,... | collective-permute-start | bytes 786440 | tf_op jit(solution)/shard_map/ppermute | solution.py:310
  72.2 3.4 %collective-permute-done.7.refs_1_ = bf16[4,32,1024]{2,1,0:T(8,128)(2,1)S(1)} collective-permute-done((bf16[4,32,1024]{2,1,0:T(8,128)(2,1)S(1)}, bf16[4,32,1024]{2,1,0:T(8,128)(2,1)S(1)}, u32[]{:S(2)}, u32[]{:S(2)}) %collective-permute-start.7) | collective-permute-done | bytes 262176 | tf_op jit(solution)/shard_map/ppermute | solution.py:310
  75.7 1.5 %collective-permute-start.9 = (bf16[4,32,1024]{2,1,0:T(8,128)(2,1)S(1)}, bf16[4,32,1024]{2,1,0:T(8,128)(2,1)S(1)}, u32[]{:S(2)}, u32[]{:S(2)}) collective-permute-start(bf16[4,32,1024]{2,1,0:T(8,128)(2,1)S(1)} %collective-permute-done.7.refs_1_), channel_id=1, source_target_pairs={{0,4},{2,6},{4,0},{6,2},{8,12},{10,14},{12,8},{14,10},{16,20},{18,... | collective-permute-start | bytes 786440 | tf_op jit(solution)/shard_map/ppermute | solution.py:310
  77.1 0.5 collective-permute-start.11
  77.6 1.6 %collective-permute-done.8.refs_2_ = bf16[4,32,1024]{2,1,0:T(8,128)(2,1)S(1)} collective-permute-done((bf16[4,32,1024]{2,1,0:T(8,128)(2,1)S(1)}, bf16[4,32,1024]{2,1,0:T(8,128)(2,1)S(1)}, u32[]{:S(2)}, u32[]{:S(2)}) %collective-permute-start.8) | collective-permute-done | bytes 262176 | tf_op jit(solution)/shard_map/ppermute | solution.py:310
  79.2 3.5 %collective-permute-done.9.refs_3_ = bf16[4,32,1024]{2,1,0:T(8,128)(2,1)S(1)} collective-permute-done((bf16[4,32,1024]{2,1,0:T(8,128)(2,1)S(1)}, bf16[4,32,1024]{2,1,0:T(8,128)(2,1)S(1)}, u32[]{:S(2)}, u32[]{:S(2)}) %collective-permute-start.9) | collective-permute-done | bytes 262176 | tf_op jit(solution)/shard_map/ppermute | solution.py:310
  82.8 1.5 %collective-permute-done.13.refs_7_ = bf16[4,32,1024]{2,1,0:T(8,128)(2,1)S(1)} collective-permute-done((bf16[4,32,1024]{2,1,0:T(8,128)(2,1)S(1)}, bf16[4,32,1024]{2,1,0:T(8,128)(2,1)S(1)}, u32[]{:S(2)}, u32[]{:S(2)}) %collective-permute-start.13) | collective-permute-done | bytes 262176 | tf_op jit(solution)/shard_map/ppermute | solution.py:451
  84.3 1.4 %assemble.1.rotation = bf16[1024,1024]{1,0:T(8,128)(2,1)S(1)} custom-call(s32[3]{0:T(128)S(1)} %pad_add_fusion.place, bf16[4,32,1024]{2,1,0:T(8,128)(2,1)S(1)} %join.1.refs_0_, bf16[4,32,1024]{2,1,0:T(8,128)(2,1)S(1)} %collective-permute-done.7.refs_1_, bf16[4,32,1024]{2,1,0:T(8,128)(2,1)S(1)} %collective-permute-done.8.refs_2_, ...), custom_call_target="tpu_custom_call" | custom-call | flops 536870912 | bytes 4194304 | tf_op jit(solution)/shard_map/assemble/pallas_call | solution.py:338
  85.7 1.6 %rotate.1 = bf16[256,1024]{1,0:T(8,128)(2,1)} custom-call(bf16[16,2,64,128]{3,2,1,0:T(8,128)(2,1)S(1)} %all-to-all-done.1.filtered, bf16[1024,1024]{1,0:T(8,128)(2,1)S(1)} %assemble.1.rotation), custom_call_target="tpu_custom_call" | custom-call | tf_op jit(solution)/shard_map/rotate/pallas_call | solution.py:379
  (14 shorter events, 0.1 us)
Async XLA Ops:
  2.8 23.4 %all-to-all-start = ((bf16[16,2,64,128]{3,2,1,0:T(8,128)(2,1)}), bf16[16,2,64,128]{3,2,1,0:T(8,128)(2,1)S(1)}, u32[]{:S(2)}, u32[]{:S(2)}) async-start(bf16[16,2,64,128]{3,2,1,0:T(8,128)(2,1)} %get-tuple-element.18), calls=%async_computation | async-start | bytes 1048576 | tf_op jit(solution)/shard_map/all_to_all | solution.py:409
  18.7 9.9 %copy-start = (s32[32,8]{0,1:T(8,128)S(1)}, s32[32,8]{0,1:T(8,128)}, u32[]{:S(2)}) copy-start(s32[32,8]{0,1:T(8,128)} %param.7) | copy-start | bytes 3076
  26.2 2.3 %collective-permute-start = (bf16[2,64,128]{2,1,0:T(8,128)(2,1)S(1)}, bf16[2,64,128]{2,1,0:T(8,128)(2,1)S(1)}, u32[]{:S(2)}, u32[]{:S(2)}) collective-permute-start(bf16[2,64,128]{2,1,0:T(8,128)(2,1)S(1)} %constant_dynamic-slice_fusion.refs_4_), channel_id=1, source_target_pairs={{0,1},{1,0},{2,3},{3,2},{4,5},{5,4},{6,7},{7,6},{8,9},{9,8},{10,11... | collective-permute-start | bytes 98312 | tf_op jit(solution)/shard_map/ppermute | solution.py:300
  32.4 1.4 %collective-permute-start.1 = (bf16[2,64,128]{2,1,0:T(8,128)(2,1)S(1)}, bf16[2,64,128]{2,1,0:T(8,128)(2,1)S(1)}, u32[]{:S(2)}, u32[]{:S(2)}) collective-permute-start(bf16[2,64,128]{2,1,0:T(8,128)(2,1)S(1)} %get-tuple-element.20), channel_id=1, source_target_pairs={{0,1},{1,0},{2,3},{3,2},{4,5},{5,4},{6,7},{7,6},{8,9},{9,8},{10,11... | collective-permute-start | bytes 98312 | tf_op jit(solution)/shard_map/ppermute | solution.py:300
  35.9 1.3 %collective-permute-start.2 = (bf16[2,64,128]{2,1,0:T(8,128)(2,1)S(1)}, bf16[2,64,128]{2,1,0:T(8,128)(2,1)S(1)}, u32[]{:S(2)}, u32[]{:S(2)}) collective-permute-start(bf16[2,64,128]{2,1,0:T(8,128)(2,1)S(1)} %get-tuple-element.24), channel_id=1, source_target_pairs={{0,1},{1,0},{2,3},{3,2},{4,5},{5,4},{6,7},{7,6},{8,9},{9,8},{10,11... | collective-permute-start | bytes 98312 | tf_op jit(solution)/shard_map/ppermute | solution.py:300
  39.3 1.3 %collective-permute-start.3 = (bf16[2,64,128]{2,1,0:T(8,128)(2,1)S(1)}, bf16[2,64,128]{2,1,0:T(8,128)(2,1)S(1)}, u32[]{:S(2)}, u32[]{:S(2)}) collective-permute-start(bf16[2,64,128]{2,1,0:T(8,128)(2,1)S(1)} %get-tuple-element.27), channel_id=1, source_target_pairs={{0,1},{1,0},{2,3},{3,2},{4,5},{5,4},{6,7},{7,6},{8,9},{9,8},{10,11... | collective-permute-start | bytes 98312 | tf_op jit(solution)/shard_map/ppermute | solution.py:300
  43.3 42.4 %all-to-all-start.1 = ((bf16[16,2,64,128]{3,2,1,0:T(8,128)(2,1)}), bf16[16,2,64,128]{3,2,1,0:T(8,128)(2,1)S(1)}, u32[]{:S(2)}, u32[]{:S(2)}) async-start(bf16[16,2,64,128]{3,2,1,0:T(8,128)(2,1)} %bitcast.15), calls=%async_computation.1 | async-start | bytes 1048576 | tf_op jit(solution)/shard_map/all_to_all | solution.py:448
  47.3 17.7 %collective-permute-start.5 = (bf16[1,32,1024]{2,1,0:T(8,128)(2,1)S(1)}, bf16[1,32,1024]{2,1,0:T(8,128)(2,1)S(1)}, u32[]{:S(2)}, u32[]{:S(2)}) collective-permute-start(bf16[1,32,1024]{2,1,0:T(8,128)(2,1)S(1)} %get-tuple-element.30.refs_0_), channel_id=1, source_target_pairs={{0,16},{2,18},{4,20},{6,22},{8,24},{10,26},{12,28},{14,30},{16,0},... | collective-permute-start | bytes 196616 | tf_op jit(solution)/shard_map/ppermute | solution.py:310
  50.1 14.9 %collective-permute-start.4 = (bf16[1,32,1024]{2,1,0:T(8,128)(2,1)S(1)}, bf16[1,32,1024]{2,1,0:T(8,128)(2,1)S(1)}, u32[]{:S(2)}, u32[]{:S(2)}) collective-permute-start(bf16[1,32,1024]{2,1,0:T(8,128)(2,1)S(1)} %get-tuple-element.30.refs_0_), channel_id=1, source_target_pairs={{0,8},{2,10},{4,12},{6,14},{8,0},{10,2},{12,4},{14,6},{16,24},{18,... | collective-permute-start | bytes 196616 | tf_op jit(solution)/shard_map/ppermute | solution.py:310
  64.9 4.3 %collective-permute-start.6 = (bf16[1,32,1024]{2,1,0:T(8,128)(2,1)S(1)}, bf16[1,32,1024]{2,1,0:T(8,128)(2,1)S(1)}, u32[]{:S(2)}, u32[]{:S(2)}) collective-permute-start(bf16[1,32,1024]{2,1,0:T(8,128)(2,1)S(1)} %collective-permute-done.5.refs_2_), channel_id=1, source_target_pairs={{0,8},{2,10},{4,12},{6,14},{8,0},{10,2},{12,4},{14,6},{16,24},{18,... | collective-permute-start | bytes 196616 | tf_op jit(solution)/shard_map/ppermute | solution.py:310
  69.2 6.4 %collective-permute-start.7 = (bf16[4,32,1024]{2,1,0:T(8,128)(2,1)S(1)}, bf16[4,32,1024]{2,1,0:T(8,128)(2,1)S(1)}, u32[]{:S(2)}, u32[]{:S(2)}) collective-permute-start(bf16[4,32,1024]{2,1,0:T(8,128)(2,1)S(1)} %join.1.refs_0_), channel_id=1, source_target_pairs={{0,2},{2,0},{4,6},{6,4},{8,10},{10,8},{12,14},{14,12},{16,18},{18,... | collective-permute-start | bytes 786440 | tf_op jit(solution)/shard_map/ppermute | solution.py:310
  70.8 8.5 %collective-permute-start.8 = (bf16[4,32,1024]{2,1,0:T(8,128)(2,1)S(1)}, bf16[4,32,1024]{2,1,0:T(8,128)(2,1)S(1)}, u32[]{:S(2)}, u32[]{:S(2)}) collective-permute-start(bf16[4,32,1024]{2,1,0:T(8,128)(2,1)S(1)} %join.1.refs_0_), channel_id=1, source_target_pairs={{0,4},{2,6},{4,0},{6,2},{8,12},{10,14},{12,8},{14,10},{16,20},{18,... | collective-permute-start | bytes 786440 | tf_op jit(solution)/shard_map/ppermute | solution.py:310
  75.7 7.1 %collective-permute-start.9 = (bf16[4,32,1024]{2,1,0:T(8,128)(2,1)S(1)}, bf16[4,32,1024]{2,1,0:T(8,128)(2,1)S(1)}, u32[]{:S(2)}, u32[]{:S(2)}) collective-permute-start(bf16[4,32,1024]{2,1,0:T(8,128)(2,1)S(1)} %collective-permute-done.7.refs_1_), channel_id=1, source_target_pairs={{0,4},{2,6},{4,0},{6,2},{8,12},{10,14},{12,8},{14,10},{16,20},{18,... | collective-permute-start | bytes 786440 | tf_op jit(solution)/shard_map/ppermute | solution.py:310
  77.1 5.6 %collective-permute-start.10 = (bf16[4,32,1024]{2,1,0:T(8,128)(2,1)S(1)}, bf16[4,32,1024]{2,1,0:T(8,128)(2,1)S(1)}, u32[]{:S(2)}, u32[]{:S(2)}) collective-permute-start(bf16[4,32,1024]{2,1,0:T(8,128)(2,1)S(1)} %join.1.refs_0_), channel_id=1, source_target_pairs={{0,1},{1,0},{2,3},{3,2},{4,5},{5,4},{6,7},{7,6},{8,9},{9,8},{10,11... | collective-permute-start | bytes 786440 | tf_op jit(solution)/shard_map/ppermute | solution.py:451
  77.1 5.6 %collective-permute-start.11 = (bf16[4,32,1024]{2,1,0:T(8,128)(2,1)S(1)}, bf16[4,32,1024]{2,1,0:T(8,128)(2,1)S(1)}, u32[]{:S(2)}, u32[]{:S(2)}) collective-permute-start(bf16[4,32,1024]{2,1,0:T(8,128)(2,1)S(1)} %collective-permute-done.7.refs_1_), channel_id=1, source_target_pairs={{0,1},{1,0},{2,3},{3,2},{4,5},{5,4},{6,7},{7,6},{8,9},{9,8},{10,11... | collective-permute-start | bytes 786440 | tf_op jit(solution)/shard_map/ppermute | solution.py:451
  79.2 3.5 %collective-permute-start.12 = (bf16[4,32,1024]{2,1,0:T(8,128)(2,1)S(1)}, bf16[4,32,1024]{2,1,0:T(8,128)(2,1)S(1)}, u32[]{:S(2)}, u32[]{:S(2)}) collective-permute-start(bf16[4,32,1024]{2,1,0:T(8,128)(2,1)S(1)} %collective-permute-done.8.refs_2_), channel_id=1, source_target_pairs={{0,1},{1,0},{2,3},{3,2},{4,5},{5,4},{6,7},{7,6},{8,9},{9,8},{10,11... | collective-permute-start | bytes 786440 | tf_op jit(solution)/shard_map/ppermute | solution.py:451
  82.7 1.5 %collective-permute-start.13 = (bf16[4,32,1024]{2,1,0:T(8,128)(2,1)S(1)}, bf16[4,32,1024]{2,1,0:T(8,128)(2,1)S(1)}, u32[]{:S(2)}, u32[]{:S(2)}) collective-permute-start(bf16[4,32,1024]{2,1,0:T(8,128)(2,1)S(1)} %collective-permute-done.9.refs_3_), channel_id=1, source_target_pairs={{0,1},{1,0},{2,3},{3,2},{4,5},{5,4},{6,7},{7,6},{8,9},{9,8},{10,11... | collective-permute-start | bytes 786440 | tf_op jit(solution)/shard_map/ppermute | solution.py:451
